TPU v7x, 512 devices: a whole 4x8x8 slice. The times are simulated.
512 devices in a mesh: blk: 16 (over z, y_lo), tan: 32 (over y_hi, x, core).
Axes of the slice: x: 4, y: 8 (y_hi: 4, y_lo: 2; y = y_hi * 2 + y_lo), z: 8, core: 2. Of those that a mesh axis runs over, the one named last changes fastest.
Arguments:
- layer_in: bfloat16 [2048, 256], P('blk'), may hold values from -6 to 6
- laplace_in: bfloat16 [2048, 256], P('blk'), may hold values from -6 to 6
- tangent_in: bfloat16 [2048, 64, 256], P('blk', 'tan'), may hold values from -1.5 to 1.5
- spin_labels: int32 [2048], P('blk'), may hold values from 0 to 1
- pair_bias: bfloat16 [2048, 2048], P('blk'), may hold values from -6 to 306
- query_weight: bfloat16 [256, 256], replicated, may hold values from -0.375 to 0.375
- key_weight: bfloat16 [256, 256], replicated, may hold values from -0.375 to 0.375
- value_weight: bfloat16 [256, 256], replicated, may hold values from -0.375 to 0.375
- out_weight: bfloat16 [256, 256], replicated, may hold values from -0.375 to 0.375
- head_gain: float32 [4], replicated, may hold values from 0.5 to 2
- spin_gain: float32 [4], replicated, may hold values from -2 to 2
Outputs:
- layer_out: bfloat16 [2048, 256], P('blk')
- tangent_out: bfloat16 [2048, 64, 256], P('blk', 'tan')
- laplacian_out: float32 [2048, 256], P('blk')
All inputs are finite; a program needn't handle non-finite values.
Results may differ from a plain program's by a relative error of at most 0.02.
Values may be sent and summed in bfloat16 or wider, within the bound.
A program may use at most 64 MiB of HBM per device.

v0:
```python
import math

import jax
import jax.numpy as jnp
from jax import lax
from jax.sharding import PartitionSpec as P


def project(rows, weight):
    return jnp.dot(rows, weight, preferred_element_type=jnp.float32).astype(jnp.bfloat16)


def project_tangent(tangent, weight):
    count, dirs, width = tangent.shape
    return project(tangent.reshape(count * dirs, width), weight).reshape(count, dirs, width)


def on_device(
    layer_in,
    laplace_in,
    tangent_in,
    spin_labels,
    pair_bias,
    query_weight,
    key_weight,
    value_weight,
    out_weight,
    head_gain,
    spin_gain,
):
    rows, width = layer_in.shape
    heads = head_gain.shape[0]
    head_size = width // heads
    dirs = tangent_in.shape[1]
    scale = 1.0 / math.sqrt(head_size)
    bias_cols = lax.all_to_all(pair_bias, "blk", split_axis=1, concat_axis=0, tiled=True)
    query = project(layer_in, query_weight).reshape(rows, heads, head_size)
    lap_query = project(laplace_in, query_weight).reshape(rows, heads, head_size)
    tan_query = project_tangent(tangent_in, query_weight).reshape(rows, dirs, heads, head_size)
    spin_query = spin_labels.astype(jnp.float32)
    spin_wire = spin_labels.astype(jnp.bfloat16)

    def attend(carry, block, first):
        top, total, numer, tan_total, tan_numer, lap_total, lap_numer, trace_total, trace_numer = (
            carry
        )
        key_b, value_b, lap_key_b, lap_value_b, tan_key_b, tan_value_b, spin_key = block
        count = key_b.shape[0]
        key_h = key_b.reshape(count, heads, head_size)
        value_h = value_b.reshape(count, heads, head_size)
        lap_key_h = lap_key_b.reshape(count, heads, head_size)
        lap_value_h = lap_value_b.reshape(count, heads, head_size)
        tan_key_h = tan_key_b.reshape(count, dirs, heads, head_size)
        tan_value_h = tan_value_b.reshape(count, dirs, heads, head_size)
        bias_rows = lax.dynamic_slice_in_dim(bias_cols, first, count, 0).astype(jnp.float32)
        spin_float = spin_key.astype(jnp.float32)
        same = (
            spin_query[:, None] * spin_float[None, :]
            + (1.0 - spin_query)[:, None] * (1.0 - spin_float)[None, :]
        )
        scores = (
            jnp.einsum("ihd,jhd->hij", query, key_h, preferred_element_type=jnp.float32) * scale
        )
        scores = (
            scores
            + head_gain[:, None, None] * bias_rows.T[None]
            + spin_gain[:, None, None] * same[None]
        )
        new_top = jnp.maximum(top, jnp.max(scores, axis=2))
        shrink = jnp.exp(top - new_top)
        shrink_rows = shrink.T[:, :, None]
        unnorm = jnp.exp(scores - new_top[:, :, None])
        weights = unnorm.astype(jnp.bfloat16)
        total = total * shrink + jnp.sum(unnorm, axis=2)
        numer = numer * shrink_rows + jnp.einsum(
            "hij,jhd->ihd", weights, value_h, preferred_element_type=jnp.float32
        )
        lap_scores = (
            jnp.einsum("ihd,jhd->hij", lap_query, key_h, preferred_element_type=jnp.float32)
            + jnp.einsum("ihd,jhd->hij", query, lap_key_h, preferred_element_type=jnp.float32)
        ) * scale
        lap_weighted = unnorm * lap_scores
        lap_total = lap_total * shrink + jnp.sum(lap_weighted, axis=2)
        lap_numer = (
            lap_numer * shrink_rows
            + jnp.einsum(
                "hij,jhd->ihd",
                lap_weighted.astype(jnp.bfloat16),
                value_h,
                preferred_element_type=jnp.float32,
            )
            + jnp.einsum("hij,jhd->ihd", weights, lap_value_h, preferred_element_type=jnp.float32)
        )
        tan_scores = (
            jnp.einsum("iahd,jhd->ahij", tan_query, key_h, preferred_element_type=jnp.float32)
            + jnp.einsum("ihd,jahd->ahij", query, tan_key_h, preferred_element_type=jnp.float32)
        ) * scale
        cross = (
            jnp.einsum("iahd,jahd->ahij", tan_query, tan_key_h, preferred_element_type=jnp.float32)
            * scale
        )
        tan_weighted = unnorm[None] * tan_scores
        tan_weights = tan_weighted.astype(jnp.bfloat16)
        tan_total = tan_total * shrink[None] + jnp.sum(tan_weighted, axis=3)
        tan_numer = (
            tan_numer * shrink_rows[:, None]
            + jnp.einsum("ahij,jhd->iahd", tan_weights, value_h, preferred_element_type=jnp.float32)
            + jnp.einsum("hij,jahd->iahd", weights, tan_value_h, preferred_element_type=jnp.float32)
        )
        second = unnorm[None] * (tan_scores * tan_scores + 2.0 * cross)
        trace_total = trace_total * shrink + jnp.sum(second, axis=(0, 3))
        trace_numer = (
            trace_numer * shrink_rows
            + jnp.einsum(
                "ahij,jhd->ihd",
                second.astype(jnp.bfloat16),
                value_h,
                preferred_element_type=jnp.float32,
            )
            + 2.0
            * jnp.einsum(
                "ahij,jahd->ihd", tan_weights, tan_value_h, preferred_element_type=jnp.float32
            )
        )
        return (
            new_top,
            total,
            numer,
            tan_total,
            tan_numer,
            lap_total,
            lap_numer,
            trace_total,
            trace_numer,
        )

    head_zeros = jnp.zeros((heads, rows), jnp.float32)
    row_zeros = jnp.zeros((rows, heads, head_size), jnp.float32)
    start_carry = (
        jnp.full((heads, rows), -1e30, jnp.float32),
        head_zeros,
        row_zeros,
        jnp.zeros((dirs, heads, rows), jnp.float32),
        jnp.zeros((rows, dirs, heads, head_size), jnp.float32),
        head_zeros,
        row_zeros,
        head_zeros,
        row_zeros,
    )
    own_keys = project(layer_in, key_weight)
    own_values = project(layer_in, value_weight)
    own_lap_keys = project(laplace_in, key_weight)
    own_lap_values = project(laplace_in, value_weight)
    own_tan_keys = project_tangent(tangent_in, key_weight)
    own_tan_values = project_tangent(tangent_in, value_weight)
    block = (
        lax.all_gather(own_keys, "blk", axis=0, tiled=True),
        lax.all_gather(own_values, "blk", axis=0, tiled=True),
        lax.all_gather(own_lap_keys, "blk", axis=0, tiled=True),
        lax.all_gather(own_lap_values, "blk", axis=0, tiled=True),
        lax.all_gather(own_tan_keys, "blk", axis=0, tiled=True),
        lax.all_gather(own_tan_values, "blk", axis=0, tiled=True),
        lax.all_gather(spin_wire, "blk", axis=0, tiled=True),
    )
    count = block[0].shape[0]
    size = 256
    parts = count // size
    stacked = tuple((piece.reshape((parts, size) + piece.shape[1:]) for piece in block))

    def step(inner, item):
        number, pieces = item
        return (attend(inner, pieces, number * size), None)

    result, _ = lax.scan(step, start_carry, (jnp.arange(parts, dtype=jnp.int32), stacked))
    top, total, numer, tan_total, tan_numer, lap_total, lap_numer, trace_total, trace_numer = result
    denom = total.T[:, :, None]
    denom_sq = denom * denom
    attn = numer / denom
    tan_denom = jnp.transpose(tan_total, (2, 0, 1))[..., None]
    attn_tan = tan_numer / denom[:, None] - numer[:, None] * tan_denom / denom_sq[:, None]
    cross_sum = jnp.sum(tan_numer * tan_denom, axis=1)
    square_sum = jnp.sum(tan_denom * tan_denom, axis=1)
    own_terms = (
        trace_numer / denom
        - numer * trace_total.T[:, :, None] / denom_sq
        - 2.0 * cross_sum / denom_sq
        + 2.0 * numer * square_sum / (denom_sq * denom)
    )
    shared = lax.psum(own_terms.reshape(rows, width).astype(jnp.bfloat16), "tan").astype(
        jnp.float32
    )
    attn_lap = (lap_numer / denom - numer * lap_total.T[:, :, None] / denom_sq).reshape(
        rows, width
    ) + shared
    layer_out = (
        jnp.dot(
            attn.reshape(rows, width).astype(jnp.bfloat16),
            out_weight,
            preferred_element_type=jnp.float32,
        )
        + layer_in.astype(jnp.float32)
    ).astype(jnp.bfloat16)
    tan_flat = attn_tan.reshape(rows * dirs, width).astype(jnp.bfloat16)
    tangent_out = jnp.dot(tan_flat, out_weight, preferred_element_type=jnp.float32).reshape(
        rows, dirs, width
    )
    tangent_out = (tangent_out + tangent_in.astype(jnp.float32)).astype(jnp.bfloat16)
    laplacian_out = jnp.dot(
        attn_lap.astype(jnp.bfloat16), out_weight, preferred_element_type=jnp.float32
    ) + laplace_in.astype(jnp.float32)
    return (layer_out, tangent_out, laplacian_out)


def solution(mesh):
    in_specs = (
        P("blk", None),
        P("blk", None),
        P("blk", "tan", None),
        P("blk"),
        P("blk", None),
        P(),
        P(),
        P(),
        P(),
        P(),
        P(),
    )
    out_specs = (P("blk", None), P("blk", "tan", None), P("blk", None))
    return jax.shard_map(
        on_device, mesh=mesh, in_specs=in_specs, out_specs=out_specs, check_vma=False
    )
```

profile of v0, /device:TPU:1, one launch (start us, length us, event | category | flops | bytes accessed | tf_op | source)
XLA Modules:
  0.0 941.4 jit_solution(8929567075966488008)
XLA Ops:
  7.2 1.8 convolution_convert_fusion.8
  9.1 1.7 convolution_convert_fusion.3
  10.9 1.7 convolution_convert_fusion.6
  12.7 1.7 convolution_convert_fusion.4
  19.4 12.0 %all-to-all-start = ((bf16[128,16,128]{2,0,1:T(8,128)(2,1)}), bf16[128,16,128]{2,0,1:T(8,128)(2,1)}, u32[]{:S(2)}, u32[]{:S(2)}) async-start(bf16[128,16,128]{2,0,1:T(8,128)(2,1)} %copy_bitcast_fusion), calls=%async_computation | async-start | bytes 1048576 | tf_op jit(solution)/shard_map/all_to_all | solution.py:36
  32.8 31.1 %all-gather = bf16[16,1,128]{2,1,0:T(2,128)(2,1)S(1)} all-gather(bf16[1,1,128]{2,1,0:T(2,128)(2,1)S(1)} %get-tuple-element.593), channel_id=1, replica_groups=mesh['blk'=16,'tan'=32] {'blk'}, dimensions={0}, use_global_device_ids=true | all-gather | bytes 4352 | tf_op jit(solution)/shard_map/all_gather | solution.py:163
  66.3 15.1 %all-gather.8.cloned.1.call-done = bf16[2048,256]{1,0:T(8,128)(2,1)} async-done(((bf16[128,256]{1,0:T(8,128)(2,1)}), bf16[2048,256]{1,0:T(8,128)(2,1)}) %all-gather.8.cloned.1.call-update) | async-done | bytes 1048592 | tf_op jit(solution)/shard_map/all_gather | solution.py:157
  81.4 74.7 %all-gather.18.cloned.1.call-done = bf16[2048,256]{1,0:T(8,128)(2,1)} async-done(((bf16[128,256]{1,0:T(8,128)(2,1)}), bf16[2048,256]{1,0:T(8,128)(2,1)}) %all-gather.18.cloned.1.call-update) | async-done | bytes 1048592 | tf_op jit(solution)/shard_map/all_gather | solution.py:160
  156.1 75.4 %all-gather.10.cloned.1.call-done = bf16[2048,256]{1,0:T(8,128)(2,1)} async-done(((bf16[128,256]{1,0:T(8,128)(2,1)}), bf16[2048,256]{1,0:T(8,128)(2,1)}) %all-gather.10.cloned.1.call-update) | async-done | bytes 1048592 | tf_op jit(solution)/shard_map/all_gather | solution.py:158
  231.5 75.2 %all-gather.16.cloned.1.call-done = bf16[2048,256]{1,0:T(8,128)(2,1)} async-done(((bf16[128,256]{1,0:T(8,128)(2,1)}), bf16[2048,256]{1,0:T(8,128)(2,1)}) %all-gather.16.cloned.1.call-update) | async-done | bytes 1048592 | tf_op jit(solution)/shard_map/all_gather | solution.py:159
  306.7 81.3 %all-gather.12.cloned.1.call-done = bf16[2048,2,256]{2,0,1:T(8,128)(2,1)} async-done(((bf16[128,2,256]{2,0,1:T(8,128)(2,1)}), bf16[2048,2,256]{2,0,1:T(8,128)(2,1)}) %all-gather.12.cloned.1.call-update) | async-done | bytes 2097168 | tf_op jit(solution)/shard_map/all_gather | solution.py:161
  388.0 79.9 %all-gather.14.cloned.1.call-done = bf16[2048,2,256]{2,0,1:T(8,128)(2,1)} async-done(((bf16[128,2,256]{2,0,1:T(8,128)(2,1)}), bf16[2048,2,256]{2,0,1:T(8,128)(2,1)}) %all-gather.14.cloned.1.call-update) | async-done | bytes 2097168 | tf_op jit(solution)/shard_map/all_gather | solution.py:162
  468.4 194.3 %while.29 = (s32[]{:T(128)}, f32[4,128]{1,0:T(4,128)S(1)}, f32[4,128]{1,0:T(4,128)}, f32[128,4,64]{0,2,1:T(8,128)}, f32[2,4,128]{2,0,1:T(2,128)S(1)}, /*index=5*...) while((s32[]{:T(128)}, f32[4,128]{1,0:T(4,128)S(1)}, ...), condition=%wide.region_7.8_spmd.clone, body=%wide.region_0.7_spmd.clone.sunk | while | flops 325065856 | bytes 26266780 | solution.py:174
  471.9 1.6 constant_dynamic-slice_fusion.10
  483.6 1.7 fusion.155
  507.9 1.8 fusion.155
  532.3 1.8 fusion.155
  556.7 1.8 fusion.155
  581.0 1.8 fusion.155
  605.4 1.8 fusion.155
  629.8 1.8 fusion.155
  654.2 1.8 fusion.155
  664.5 1.8 add_convert_fusion
  669.2 263.7 %all-reduce.2.cloned.1.call-done = bf16[128,256]{0,1:T(8,128)(2,1)} async-done(((bf16[128,256]{0,1:T(8,128)(2,1)}), bf16[128,256]{0,1:T(8,128)(2,1)}) %all-reduce.2.cloned.1.call-update) | async-done | bytes 65552 | tf_op jit(solution)/shard_map/psum | solution.py:189
  (493 shorter events, 187.0 us)
Async XLA Ops:
  7.2 11.3 %copy-start = (bf16[128,2048]{1,0:T(8,128)(2,1)S(1)}, bf16[128,2048]{1,0:T(8,128)(2,1)}, u32[]{:S(2)}) copy-start(bf16[128,2048]{1,0:T(8,128)(2,1)} %param.17) | copy-start | bytes 1572868
  7.2 10.3 %copy-start.5 = (bf16[256,256]{1,0:T(8,128)(2,1)S(1)}, bf16[256,256]{1,0:T(8,128)(2,1)}, u32[]{:S(2)}) copy-start(bf16[256,256]{1,0:T(8,128)(2,1)} %param.20) | copy-start | bytes 393220
  7.2 74.2 %all-gather.8.cloned.1.call-start = ((), (), s32[]{:S(2)}) async-start(), calls=%async_computation.1 | async-start | bytes 1114112 | tf_op jit(solution)/shard_map/all_gather | solution.py:157
  9.1 147.0 %all-gather.18.cloned.1.call-start = ((), (), s32[]{:S(2)}) async-start(), calls=%async_computation.6 | async-start | bytes 1114112 | tf_op jit(solution)/shard_map/all_gather | solution.py:160
  10.9 220.6 %all-gather.10.cloned.1.call-start = ((), (), s32[]{:S(2)}) async-start(), calls=%async_computation.2 | async-start | bytes 1114112 | tf_op jit(solution)/shard_map/all_gather | solution.py:158
  12.7 294.0 %all-gather.16.cloned.1.call-start = ((), (), s32[]{:S(2)}) async-start(), calls=%async_computation.5 | async-start | bytes 1114112 | tf_op jit(solution)/shard_map/all_gather | solution.py:159
  14.5 373.5 %all-gather.12.cloned.1.call-start = ((), (), s32[]{:S(2)}) async-start(), calls=%async_computation.3 | async-start | bytes 2228224 | tf_op jit(solution)/shard_map/all_gather | solution.py:161
  15.5 16.1 %copy-start.6 = (bf16[256,256]{1,0:T(8,128)(2,1)S(1)}, bf16[256,256]{1,0:T(8,128)(2,1)}, u32[]{:S(2)}) copy-start(bf16[256,256]{1,0:T(8,128)(2,1)} %param.18) | copy-start | bytes 393220
  17.4 15.4 %copy-start.18 = (s32[128]{0:T(128)S(1)}, s32[128]{0:T(128)}, u32[]{:S(2)}) copy-start(s32[128]{0:T(128)} %param.16) | copy-start | bytes 1540
  17.4 47.1 %copy-start.8 = (bf16[128,256]{1,0:T(8,128)(2,1)S(1)}, bf16[128,256]{1,0:T(8,128)(2,1)}, u32[]{:S(2)}) copy-start(bf16[128,256]{1,0:T(8,128)(2,1)} %param.13) | copy-start | bytes 196612
  17.4 450.4 %all-gather.14.cloned.1.call-start = ((), (), s32[]{:S(2)}) async-start(), calls=%async_computation.4 | async-start | bytes 2228224 | tf_op jit(solution)/shard_map/all_gather | solution.py:162
  17.8 47.7 %copy-start.10 = (bf16[128,256]{1,0:T(8,128)(2,1)S(1)}, bf16[128,256]{1,0:T(8,128)(2,1)}, u32[]{:S(2)}) copy-start(bf16[128,256]{1,0:T(8,128)(2,1)} %param.14) | copy-start | bytes 196612
  19.4 46.9 %all-to-all-start = ((bf16[128,16,128]{2,0,1:T(8,128)(2,1)}), bf16[128,16,128]{2,0,1:T(8,128)(2,1)}, u32[]{:S(2)}, u32[]{:S(2)}) async-start(bf16[128,16,128]{2,0,1:T(8,128)(2,1)} %copy_bitcast_fusion), calls=%async_computation | async-start | bytes 1048576 | tf_op jit(solution)/shard_map/all_to_all | solution.py:36
  31.4 901.4 %all-reduce.2.cloned.1.call-start = ((), (), s32[]{:S(2)}) async-start(), calls=%async_computation.7 | async-start | bytes 131072 | tf_op jit(solution)/shard_map/psum | solution.py:189
  482.1 6.7 copy-start.4
  492.0 5.2 copy-start.16
  505.7 7.5 copy-start.4
  530.1 7.5 copy-start.4
  554.5 7.5 copy-start.4
  578.8 7.5 copy-start.4
  603.2 7.5 copy-start.4
  627.6 7.5 copy-start.4
  651.9 7.5 copy-start.4
  662.6 271.1 %copy-start.11 = (bf16[128,256]{1,0:T(8,128)(2,1)S(1)}, bf16[128,256]{1,0:T(8,128)(2,1)}, u32[]{:S(2)}) copy-start(bf16[128,256]{1,0:T(8,128)(2,1)} %param.14) | copy-start | bytes 196612
  (73 other events, 147.2 us)
Sparse Core Ops, SparseCore 0:
  10.7 70.6 all-gather.7
  83.5 72.5 all-gather.17
  158.2 73.2 all-gather.9
  233.4 73.2 all-gather.15
  308.6 79.3 all-gather.11
  389.9 77.8 all-gather.13
  666.4 266.3 all-reduce.1
where the time goes:
time: 947 us; the launch traced here: 941 us
  waiting for transfers between devices  665 us (70%)
  matrix products  112 us (12%)
  local copies, waits for them, and re-layouts  65 us (7%)
  other arithmetic  34.7 us (4%)
  blocking collectives  31.1 us (3%)
  between operations  14.4 us (2%)
  starting transfers between devices  12.3 us (1%)
    psum x1, waiting for transfers between devices, on_device(): lax.psum(own_terms.reshape(rows, width).astype(jnp.bfloat16), 'tan')  264 us
    all_gather x1, waiting for transfers between devices, on_device(): lax.all_gather(own_tan_keys, 'blk', axis=0, tiled=True)  81.3 us
    all_gather x1, waiting for transfers between devices, on_device(): lax.all_gather(own_tan_values, 'blk', axis=0, tiled=True)  79.9 us
    all_gather x1, waiting for transfers between devices, on_device(): lax.all_gather(own_values, 'blk', axis=0, tiled=True)  75.4 us
    all_gather x1, waiting for transfers between devices, on_device(): lax.all_gather(own_lap_keys, 'blk', axis=0, tiled=True)  75.2 us
    all_gather x1, waiting for transfers between devices, on_device(): lax.all_gather(own_lap_values, 'blk', axis=0, tiled=True)  74.7 us
    dynamic_slice x80, local copies, waits for them, and re-layouts, on_device(): lax.scan(step, start_carry, (jnp.arange(parts, dtype=jnp.int32), stacked))  52.4 us
    all_gather x1, blocking collectives, on_device(): lax.all_gather(spin_wire, 'blk', axis=0, tiled=True)  31.1 us
  transfers between devices with their start and end apart: 8, of which 7 were waited for; matrix products, arithmetic and copies ran while one was open for 2% of the time, Pallas kernels for 0%

commit v1 on v0

v1 whole, which is shorter than its diff:
```python
import functools

import jax
import jax.numpy as jnp
from jax import lax
from jax.experimental import pallas as pl
from jax.experimental.pallas import tpu as pltpu
from jax.sharding import PartitionSpec as P

MESH = pl.DeviceIdType.MESH
F32 = jnp.float32
BF16 = jnp.bfloat16
ROWS = 128
HALF = 64
WIDTH = 256
HEADS = 4
HEAD = 64
CORES = 2


def dot(a, b):
    return jnp.dot(a, b, preferred_element_type=F32)


def dot_t(a, b):
    return lax.dot_general(a, b, (((1,), (1,)), ((), ())), preferred_element_type=F32)


def kernel(
    nz,
    tans,
    layer_hbm,
    lap_hbm,
    tan_hbm,
    spin_hbm,
    bias_hbm,
    wq_hbm,
    wk_hbm,
    wv_hbm,
    wo_hbm,
    hg_ref,
    sg_ref,
    layer_out,
    tan_out,
    lap_out,
    wq,
    wk,
    wv,
    wo,
    wvt,
    lap_own,
    spin_own,
    g_l,
    g_t,
    g_r,
    g_b,
    g_s,
    g_x,
    qa,
    qb,
    qc,
    ql,
    kk,
    vt,
    s_bias,
    s_same,
    s_spin,
    top_ref,
    acc,
    sums,
    a_attn,
    a_tan,
    own,
    rs,
    red,
    ag,
    local_sem,
    t_z_send,
    t_z_recv,
    t_y_send,
    t_y_recv,
    l_z_send,
    l_z_recv,
    l_y_send,
    l_y_recv,
    l_c_send,
    l_c_recv,
    r_z_send,
    r_z_recv,
    r_y_send,
    r_y_recv,
    b_d_send,
    b_d_recv,
    b_c_send,
    b_c_recv,
    s_send,
    s_recv,
    x_send,
    x_recv,
    rs_send,
    rs_recv,
    ag_send,
    ag_recv,
):
    blk = lax.axis_index("blk")
    tan = lax.axis_index("tan")
    blks = 2 * nz
    z = blk // 2
    y = blk % 2
    core = tan % 2
    my_half = pl.ds(pl.multiple_of(core * HALF, HALF), HALF)

    barrier = pltpu.get_barrier_semaphore()

    def greet_blk(k, carry):
        pl.semaphore_signal(
            barrier, inc=1, device_id={"blk": (blk + k) % blks}, device_id_type=MESH
        )
        return carry

    def greet_tan(k, carry):
        pl.semaphore_signal(
            barrier, inc=1, device_id={"tan": (tan + k) % tans}, device_id_type=MESH
        )
        return carry

    lax.fori_loop(1, blks, greet_blk, 0)
    lax.fori_loop(1, tans, greet_tan, 0)

    own_cols = pl.ds(pl.multiple_of(blk * ROWS, ROWS), ROWS)
    local = [
        (tan_hbm.at[0], g_t.at[0, 0]),
        (layer_hbm, g_l.at[0, 0]),
        (tan_hbm.at[1], g_r.at[0, 0]),
        (wq_hbm, wq),
        (wk_hbm, wk),
        (wv_hbm, wv),
        (lap_hbm, lap_own),
        (spin_hbm, spin_own),
        (bias_hbm.at[:, own_cols], g_b.at[0, 0]),
        (wo_hbm, wo),
    ]
    local = [
        pltpu.make_async_copy(src, dst, local_sem.at[n]) for n, (src, dst) in enumerate(local)
    ]
    for copy in local:
        copy.start()

    up_z = {"blk": ((z + 1) % nz) * 2 + y}
    down_z = {"blk": ((z + nz - 1) % nz) * 2 + y}
    other_y = {"blk": z * 2 + (1 - y)}
    other_core = {"tan": tan + 1 - 2 * core}

    started = []

    def remote(src, dst, send, recv, device):
        return pltpu.make_async_remote_copy(
            src_ref=src,
            dst_ref=dst,
            send_sem=send,
            recv_sem=recv,
            device_id=device,
            device_id_type=MESH,
        )

    def before(o, up):
        return (o - 1, up_z) if up else ((o + 1) % nz, down_z)

    last_up = nz // 2
    last_up_r = nz - 1 - last_up

    def flow_t(o):
        src, device = before(o, o <= last_up)
        return remote(g_t.at[src, 0], g_t.at[o, 0], t_z_send.at[o], t_z_recv.at[o], device)

    def flow_l(o):
        src, device = before(o, o <= last_up)
        return remote(
            g_l.at[src, 0, my_half],
            g_l.at[o, 0, my_half],
            l_z_send.at[o],
            l_z_recv.at[o],
            device,
        )

    def flow_r(o, side):
        src, device = before(o, o <= last_up_r)
        return remote(
            g_r.at[src, side],
            g_r.at[o, side],
            r_z_send.at[o, side],
            r_z_recv.at[o, side],
            device,
        )

    def cross_t(o):
        return remote(g_t.at[o, 0], g_t.at[o, 1], t_y_send.at[o], t_y_recv.at[o], other_y)

    def cross_l(o):
        return remote(
            g_l.at[o, 0, my_half],
            g_l.at[o, 1, my_half],
            l_y_send.at[o],
            l_y_recv.at[o],
            other_y,
        )

    cross_r = remote(g_r.at[0, 0], g_r.at[0, 1], r_y_send.at[0], r_y_recv.at[0], other_y)

    def mate_l(o, side):
        return remote(
            g_l.at[o, side, my_half],
            g_l.at[o, side, my_half],
            l_c_send.at[o, side],
            l_c_recv.at[o, side],
            other_core,
        )

    def mate_b(o, side):
        return remote(
            g_b.at[o, side, my_half],
            g_b.at[o, side, my_half],
            b_c_send.at[o, side],
            b_c_recv.at[o, side],
            other_core,
        )

    def peer(o, side):
        return ((z + o) % nz) * 2 + (y + side) % 2

    def direct_b(o, side):
        there = peer(o, side)
        columns = pl.ds(pl.multiple_of(there * ROWS, ROWS), ROWS)
        return remote(
            bias_hbm.at[my_half, columns],
            g_b.at[o, side, my_half],
            b_d_send.at[o, side],
            b_d_recv.at[o, side],
            {"blk": there},
        )

    def direct_s(o, side):
        return remote(
            spin_hbm,
            g_s.at[o, side],
            s_send.at[o, side],
            s_recv.at[o, side],
            {"blk": peer(o, side)},
        )

    def start(copy):
        copy.start()
        started.append(copy)

    def next_of(o, last):
        if o == 0:
            return [n for n in (1, nz - 1) if n in arrivals(1, last)]
        if o <= last:
            return [o + 1] if o < last else []
        return [o - 1] if o - 1 > last else []

    def arrivals(step, last):
        found = [step] if step <= last else []
        down = nz - step
        if down > last and down != step or (down == step and step > last):
            found.append(down)
        return found

    share_o = tan // 4
    share_y = (tan // 2) % 2
    is_own = tan < 2
    share_to = ((z + share_o) % nz) * 2 + (y + share_y) % 2
    copy_x = remote(lap_hbm.at[my_half], g_x, x_send.at[0], x_recv.at[0], {"blk": share_to})
    copy_x_own = pltpu.make_async_copy(lap_hbm.at[my_half], g_x, local_sem.at[10])

    for copy in local[:3]:
        copy.wait()
    pl.semaphore_wait(barrier, blks - 1 + tans - 1)

    for o in next_of(0, last_up):
        start(flow_t(o))
    start(cross_t(0))
    for o in next_of(0, last_up):
        start(flow_l(o))
    start(cross_r)
    start(cross_l(0))
    for o in next_of(0, last_up_r):
        start(flow_r(o, 0))
    order = [0]
    for step in range(1, nz // 2 + 1):
        order += sorted({step, nz - step})
    for o in order:
        for side in (0, 1):
            if (o, side) != (0, 0):
                start(direct_s(o, side))
                start(direct_b(o, side))

    @pl.when(is_own)
    def _():
        copy_x_own.start()

    @pl.when(jnp.logical_not(is_own))
    def _():
        copy_x.start()

    for copy in local[3:]:
        copy.wait()

    wvt[...] = jnp.transpose(wv[...].astype(F32)).astype(BF16)
    lanes = lax.broadcasted_iota(jnp.int32, (ROWS, ROWS), 1)

    def queries(rows):
        return dot(rows, wq[...]).astype(BF16).astype(F32) * 0.125

    q = queries(g_l[0, 0])
    q0 = queries(g_t[0, 0])
    q1 = queries(g_r[0, 0])
    qlap = queries(lap_own[...])
    for pair in range(2):
        cols = slice(pair * ROWS, (pair + 1) * ROWS)
        for e in range(2):
            keep = (lanes >= e * HEAD) & (lanes < (e + 1) * HEAD)

            def part(value, scale=1.0):
                return jnp.where(keep, value[:, cols] * scale, 0.0).astype(BF16)

            first = slice(e * ROWS, (e + 1) * ROWS)
            second = slice((2 + e) * ROWS, (3 + e) * ROWS)
            left, right = slice(0, ROWS), slice(ROWS, 2 * ROWS)
            zero = jnp.zeros((ROWS, ROWS), BF16)
            qa[pair, first, left] = part(q)
            qa[pair, first, right] = zero
            qa[pair, second, left] = part(q0)
            qa[pair, second, right] = part(q)
            qb[pair, first, left] = part(q1)
            qb[pair, first, right] = part(q)
            qc[pair, first, left] = part(q0, 2.0)
            qc[pair, first, right] = part(q1, 2.0)
            ql[pair, first, left] = part(q)
            ql[pair, first, right] = zero
            ql[pair, second, left] = part(qlap)
            ql[pair, second, right] = part(q)

    for h in range(HEADS):
        vt[h, 3 * HEAD :, :] = jnp.ones((16, 2 * ROWS), BF16)
    top_ref[...] = jnp.full(top_ref.shape, -1e30, F32)
    acc[...] = jnp.zeros(acc.shape, F32)
    sums[...] = jnp.zeros(sums.shape, F32)
    g_s[0, 0] = spin_own[...]
    spin_row = spin_own[...]

    def same_as(o, side):
        keys = jnp.transpose(jnp.broadcast_to(g_s[o, side], (ROWS, ROWS)))
        return jnp.where(keys == spin_row, 1.0, 0.0)

    def attend(o):
        x = g_l[o].reshape(2 * ROWS, WIDTH)
        x0 = g_t[o].reshape(2 * ROWS, WIDTH)
        x1 = g_r[o].reshape(2 * ROWS, WIDTH)
        for n, rows in enumerate((x, x0, x1)):
            keys = dot(rows, wk[...]).astype(BF16)
            for pair in range(2):
                kk[pair, n] = keys[:, pair * ROWS : (pair + 1) * ROWS]
            values = dot_t(wvt[...], rows).astype(BF16)
            place = (1, 0, 2)[n] * HEAD
            for h in range(HEADS):
                vt[h, place : place + HEAD, :] = values[h * HEAD : (h + 1) * HEAD]
        for side in range(2):
            rows = slice(side * ROWS, (side + 1) * ROWS)
            s_bias[rows] = g_b[o, side].astype(F32)
            s_same[rows] = same_as(o, side)

        def pair_step(pair, carry):
            k, k0, k1 = kk[pair, 0], kk[pair, 1], kk[pair, 2]
            ra = dot_t(jnp.concatenate([k, k0], 1), qa[pair])
            rb = dot_t(jnp.concatenate([k, k1], 1), qb[pair])
            rc = dot_t(jnp.concatenate([k0, k1], 1), qc[pair])
            for e in range(2):
                h = pair * 2 + e
                one = slice(e * ROWS, (e + 1) * ROWS)
                two = slice((2 + e) * ROWS, (3 + e) * ROWS)
                scores = ra[:, one] + hg_ref[h] * s_bias[...] + sg_ref[h] * s_same[...]
                t0, t1, c = ra[:, two], rb[:, one], rc[:, one]
                old = top_ref[h]
                top = jnp.maximum(old, jnp.max(scores, axis=0, keepdims=True))
                top_ref[h] = top
                shrink = jnp.exp(old - top)
                expo = jnp.exp(scores - top)
                e0 = expo * t0
                e1 = expo * t1
                e2 = e0 * t0 + e1 * t1 + expo * c
                w = expo.astype(BF16)
                w0 = e0.astype(BF16)
                w1 = e1.astype(BF16)
                w2 = e2.astype(BF16)
                p = dot(vt[h], jnp.concatenate([w, w0], 1))
                r = dot(vt[h, HEAD:, :], jnp.concatenate([w1, w2], 1))
                left, right = slice(0, ROWS), slice(ROWS, 2 * ROWS)
                a, b, d = slice(0, 64), slice(64, 128), slice(128, 192)
                acc[h, 0:64] = acc[h, 0:64] * shrink + p[b, left]
                acc[h, 64:128] = acc[h, 64:128] * shrink + (p[b, right] + p[a, left])
                acc[h, 128:192] = acc[h, 128:192] * shrink + (r[a, left] + p[d, left])
                acc[h, 192:256] = acc[h, 192:256] * shrink + (
                    r[a, right] + 2.0 * (p[a, right] + r[b, left])
                )
                sums[h, 0] = sums[h, 0] * shrink + p[192:200, left]
                sums[h, 1] = sums[h, 1] * shrink + p[192:200, right]
                sums[h, 2] = sums[h, 2] * shrink + r[128:136, left]
                sums[h, 3] = sums[h, 3] * shrink + r[128:136, right]
            return carry

        lax.fori_loop(0, 2, pair_step, 0)

    def offsets(step):
        return [step] if step == nz - step or step == 0 else [step, nz - step]

    def ring(step):
        if step == 0:
            cross_r.wait_recv()
            for o in next_of(0, last_up_r):
                start(flow_r(o, 1))
            return
        for o in arrivals(step, last_up):
            flow_t(o).wait_recv()
            for n in next_of(o, last_up):
                start(flow_t(n))
            start(cross_t(o))
            flow_l(o).wait_recv()
            for n in next_of(o, last_up):
                start(flow_l(n))
            start(cross_l(o))
            start(mate_l(o, 0))
        for side in range(2):
            for o in arrivals(step, last_up_r):
                flow_r(o, side).wait_recv()
                for n in next_of(o, last_up_r):
                    start(flow_r(n, side))

    def share(step):
        for o in offsets(step):
            cross_l(o).wait_recv()
            start(mate_l(o, 1))
            for side in range(2):
                if (o, side) != (0, 0):
                    direct_b(o, side).wait_recv()
                    start(mate_b(o, side))

    def use(step):
        for o in offsets(step):
            cross_t(o).wait_recv()
            for side in range(2):
                if (o, side) != (0, 0):
                    mate_l(o, side).wait_recv()
                    mate_b(o, side).wait_recv()
                    direct_s(o, side).wait_recv()
        choices = offsets(step)
        if len(choices) == 1:
            attend(choices[0])
        else:
            jump = choices[1] - choices[0]

            def one(n, carry):
                attend(choices[0] + n * jump)
                return carry

            lax.fori_loop(0, 2, one, 0)

    steps = nz // 2
    for step in range(steps + 1):
        ring(step)
        if step >= 1:
            share(step - 1)
        if step >= 2:
            use(step - 2)
    share(steps)
    use(steps - 1)
    use(steps)

    @pl.when(is_own)
    def _():
        copy_x_own.wait()

    @pl.when(jnp.logical_not(is_own))
    def _():
        copy_x.wait()

    lx = g_l[share_o, share_y, my_half]
    lk = dot(lx, wk[...]).astype(BF16)
    lv = dot_t(wvt[...], lx).astype(BF16)
    lk2 = dot(g_x[...], wk[...]).astype(BF16)
    lv2 = dot_t(wvt[...], g_x[...]).astype(BF16)
    lbias = g_b[share_o, share_y, my_half].astype(F32)
    s_spin[...] = same_as(share_o, share_y)
    lsame = s_spin[my_half]
    for pair in range(2):
        cols = slice(pair * ROWS, (pair + 1) * ROWS)
        res = dot_t(jnp.concatenate([lk[:, cols], lk2[:, cols]], 1), ql[pair])
        for e in range(2):
            h = pair * 2 + e
            scores = res[:, e * ROWS : (e + 1) * ROWS] + hg_ref[h] * lbias + sg_ref[h] * lsame
            expo = jnp.exp(scores - top_ref[h])
            w = expo.astype(BF16)
            wl = (expo * res[:, (2 + e) * ROWS : (3 + e) * ROWS]).astype(BF16)
            hrows = slice(h * HEAD, (h + 1) * HEAD)
            lnum = dot(lv[hrows], wl) + dot(lv2[hrows], w)
            lsum = jnp.sum(wl.astype(F32), axis=0, keepdims=True)
            inv = 1.0 / sums[h, 0, 0:1]
            td0 = sums[h, 1, 0:1]
            td1 = sums[h, 2, 0:1]
            trd = sums[h, 3, 0:1] + lsum
            attn = acc[h, 0:64] * inv
            at0 = (acc[h, 64:128] - attn * td0) * inv
            at1 = (acc[h, 128:192] - attn * td1) * inv
            term = (acc[h, 192:256] + lnum - attn * trd - 2.0 * (td0 * at0 + td1 * at1)) * inv
            a_attn[hrows] = attn
            a_tan[0, hrows] = at0
            a_tan[1, hrows] = at1
            own[h * 8 : (h + 1) * 8] = term.reshape(8, 8, ROWS)

    def rs_copy(k):
        there = (tan + k) % tans
        return remote(own.at[there], rs.at[k], rs_send.at[k], rs_recv.at[k], {"tan": there})

    def ag_copy(k):
        there = (tan + k) % tans
        return remote(red, ag.at[tan], ag_send.at[k], ag_recv.at[k], {"tan": there})

    def each(body):
        def run(k, carry):
            body(k)
            return carry

        lax.fori_loop(1, tans, run, 0)

    each(lambda k: rs_copy(k).start())

    def project_out(value, rows):
        flat = jnp.transpose(value).astype(BF16)
        return dot(flat, wo[...]) + rows.astype(F32)

    layer_out[...] = project_out(a_attn[...], g_l[0, 0]).astype(BF16)
    tan_out[0] = project_out(a_tan[0], g_t[0, 0]).astype(BF16)
    tan_out[1] = project_out(a_tan[1], g_r[0, 0]).astype(BF16)
    rs[0] = own[tan]

    each(lambda k: rs_copy(k).wait_recv())
    red[...] = jnp.sum(rs[...], axis=0)
    each(lambda k: ag_copy(k).start())
    ag[tan] = red[...]
    each(lambda k: rs_copy(k).wait_send())
    for copy in started:
        copy.wait_send()
    each(lambda k: ag_copy(k).wait_recv())
    lap_out[...] = project_out(ag[...].reshape(WIDTH, ROWS), lap_own[...])
    each(lambda k: ag_copy(k).wait_send())


def solution(mesh):
    blks, tans = mesh.shape["blk"], mesh.shape["tan"]
    nz = blks // 2

    def on_device(layer, lap, tangent, spin, bias, wq, wk, wv, wo, hg, sg):
        tangents = jnp.transpose(tangent, (1, 0, 2))
        spins = spin.astype(F32).reshape(1, ROWS)
        any_spec = pl.BlockSpec(memory_space=pl.ANY)
        smem = pl.BlockSpec(memory_space=pltpu.SMEM)
        vmem = pl.BlockSpec(memory_space=pltpu.VMEM)
        sq = (WIDTH, WIDTH)
        scratch = [
            pltpu.VMEM(sq, BF16),
            pltpu.VMEM(sq, BF16),
            pltpu.VMEM(sq, BF16),
            pltpu.VMEM(sq, BF16),
            pltpu.VMEM(sq, BF16),
            pltpu.VMEM((ROWS, WIDTH), BF16),
            pltpu.VMEM((1, ROWS), F32),
            pltpu.VMEM((nz, 2, ROWS, WIDTH), BF16),
            pltpu.VMEM((nz, 2, ROWS, WIDTH), BF16),
            pltpu.VMEM((nz, 2, ROWS, WIDTH), BF16),
            pltpu.VMEM((nz, 2, ROWS, ROWS), BF16),
            pltpu.VMEM((nz, 2, 1, ROWS), F32),
            pltpu.VMEM((HALF, WIDTH), BF16),
            pltpu.VMEM((2, 4 * ROWS, WIDTH), BF16),
            pltpu.VMEM((2, 2 * ROWS, WIDTH), BF16),
            pltpu.VMEM((2, 2 * ROWS, WIDTH), BF16),
            pltpu.VMEM((2, 4 * ROWS, WIDTH), BF16),
            pltpu.VMEM((2, 3, 2 * ROWS, ROWS), BF16),
            pltpu.VMEM((HEADS, 3 * HEAD + 16, 2 * ROWS), BF16),
            pltpu.VMEM((2 * ROWS, ROWS), F32),
            pltpu.VMEM((2 * ROWS, ROWS), F32),
            pltpu.VMEM((ROWS, ROWS), F32),
            pltpu.VMEM((HEADS, 1, ROWS), F32),
            pltpu.VMEM((HEADS, 4 * HEAD, ROWS), F32),
            pltpu.VMEM((HEADS, 4, 8, ROWS), F32),
            pltpu.VMEM((WIDTH, ROWS), F32),
            pltpu.VMEM((2, WIDTH, ROWS), F32),
            pltpu.VMEM((tans, WIDTH // tans, ROWS), F32),
            pltpu.VMEM((tans, WIDTH // tans, ROWS), F32),
            pltpu.VMEM((WIDTH // tans, ROWS), F32),
            pltpu.VMEM((tans, WIDTH // tans, ROWS), F32),
            pltpu.SemaphoreType.DMA((11,)),
        ]
        one, two = (nz,), (nz, 2)
        for shape in (one, one, one, one, two, two, (1,), two, two, two, (1,), (tans,), (tans,)):
            scratch += [pltpu.SemaphoreType.DMA(shape)] * 2
        layer_out, tan_out, lap_out = pl.pallas_call(
            functools.partial(kernel, nz, tans),
            out_shape=(
                jax.ShapeDtypeStruct((ROWS, WIDTH), BF16),
                jax.ShapeDtypeStruct((2, ROWS, WIDTH), BF16),
                jax.ShapeDtypeStruct((ROWS, WIDTH), F32),
            ),
            in_specs=[any_spec] * 9 + [smem, smem],
            out_specs=(vmem, vmem, vmem),
            scratch_shapes=scratch,
            compiler_params=pltpu.CompilerParams(collective_id=0, has_side_effects=True),
            name="laplacian_attention",
        )(layer, lap, tangents, spins, bias, wq, wk, wv, wo, hg, sg)
        return layer_out, jnp.transpose(tan_out, (1, 0, 2)), lap_out

    in_specs = (
        P("blk", None),
        P("blk", None),
        P("blk", "tan", None),
        P("blk"),
        P("blk", None),
        P(),
        P(),
        P(),
        P(),
        P(),
        P(),
    )
    out_specs = (P("blk", None), P("blk", "tan", None), P("blk", None))
    return jax.shard_map(
        on_device, mesh=mesh, in_specs=in_specs, out_specs=out_specs, check_vma=False
    )
```

time: 947 us -> 80.8 us (0.09)
  waiting for transfers between devices: 665 us -> 0 us
  matrix products: 112 us -> 0 us
  Pallas kernels: 0 us -> 73.9 us
  local copies, waits for them, and re-layouts: 65 us -> 4.89 us
  other arithmetic: 34.7 us -> 1.17 us
  blocking collectives: 31.1 us -> 0 us
  between operations: 14.4 us -> 0.65 us
  starting transfers between devices: 12.3 us -> 0 us
    all_gather x6 -> x0, waiting for transfers between devices: 402 us -> none  [the longest x1 81.3 us: on_device(): lax.all_gather(own_tan_keys, 'blk', axis=0, tiled=True)]
    psum x1 -> x0, waiting for transfers between devices: 264 us -> none  [on_device(): lax.psum(own_terms.reshape(rows, width).astype(jnp.bfloat16), 'tan')]
    dot_general x116 -> x0, matrix products: 112 us -> none  [the longest x8 14.4 us: attend(): jnp.einsum('ahij,jhd->ihd', second.astype(jnp.bfloat16), value_h, preferr...]
    pallas_call x0 -> x1, Pallas kernels: none -> 73.9 us  [on_device(): pl.pallas_call(functools.partial(kernel, nz, tans), out_shape=(jax.ShapeD...]
    dynamic_slice x80 -> x0, local copies, waits for them, and re-layouts: 52.4 us -> none  [on_device(): lax.scan(step, start_carry, (jnp.arange(parts, dtype=jnp.int32), stacked))]
    all_gather x1 -> x0, blocking collectives: 31.1 us -> none  [on_device(): lax.all_gather(spin_wire, 'blk', axis=0, tiled=True)]
    all_to_all x1 -> x0, starting transfers between devices: 12 us -> none  [on_device(): lax.all_to_all(pair_bias, 'blk', split_axis=1, concat_axis=0, tiled=True)]
    add x32 -> x0, other arithmetic: 10.3 us -> none  [the longest x8 9.01 us: attend(): trace_total = trace_total * shrink + jnp.sum(second, axis=(0, 3))]
  transfers between devices with their start and end apart: 8 -> 0, of which waited for: 7 -> 0; matrix products, arithmetic and copies ran while one was open for 2% -> 0% of each run, Pallas kernels for 0% -> 0%
where the time goes in v1:
time: 80.8 us; the launch traced here: 80.6 us
  Pallas kernels  73.9 us (91%)
  local copies, waits for them, and re-layouts  4.89 us (6%)
  other arithmetic  1.17 us (1%)
    pallas_call x1, Pallas kernels, on_device(): pl.pallas_call(functools.partial(kernel, nz, tans), out_shape=(jax.ShapeD...  73.9 us
    unnamed x8, local copies, waits for them, and re-layouts  4.89 us

profile of v1, /device:TPU:1, one launch (start us, length us, event | category | flops | bytes accessed | tf_op | source)
XLA Modules:
  0.0 80.6 jit_solution(13956276701679951154)
XLA Ops:
  0.6 1.2 %convert_bitcast_fusion.spin_hbm = f32[1,128]{1,0:T(1,128)} fusion(s32[128]{0:T(128)} %param.14), kind=kLoop, calls=%fused_computation.1 | loop fusion | flops 128 | bytes 1024 | tf_op jit(solution)/shard_map/reshape | solution.py:564
  1.8 1.6 %copy.17 = bf16[128,2,256]{2,0,1:T(8,128)(2,1)} copy(bf16[128,2,256]{2,1,0:T(2,128)(2,1)} %param.13) | data formatting | bytes 262144 | tf_op args[2]
  3.4 73.9 %laplacian_attention.1 = (bf16[128,256]{1,0:T(8,128)(2,1)}, bf16[2,128,256]{2,1,0:T(8,128)(2,1)}, f32[128,256]{1,0:T(8,128)}) custom-call(bf16[128,256]{1,0:T(8,128)(2,1)} %layer_hbm.1, bf16[128,256]{1,0:T(8,128)(2,1)} %lap_hbm.1, bf16[2,128,256]{2,1,0:T(8,128)(2,1)} %bitcast.6, f32[1,128]{1,0:T(1,128)} %convert_bitcast_fusion.spin_hbm, ...), custom_call_target="tpu_custom_call" | custom-call | tf_op jit(solution)/shard_map/laplacian_attention/pallas_call | solution.py:606
  77.3 0.0 copy-start.1
  77.3 1.7 %copy.15 = bf16[128,2,256]{2,1,0:T(2,128)(2,1)} copy(bf16[128,2,256]{2,0,1:T(8,128)(2,1)} %bitcast.7) | data formatting | bytes 262144
  79.0 0.0 copy-done.1
  79.1 0.0 copy-start
  79.1 0.6 copy.20
  79.7 0.3 copy-done
  80.0 0.7 copy.21
Async XLA Ops:
  77.3 1.7 %copy-start.1 = (bf16[128,256]{1,0:T(8,128)(2,1)S(1)}, bf16[128,256]{1,0:T(8,128)(2,1)}, u32[]{:S(2)}) copy-start(bf16[128,256]{1,0:T(8,128)(2,1)} %get-tuple-element.15) | copy-start | bytes 196612
  79.1 0.9 %copy-start = (f32[128,256]{1,0:T(8,128)S(1)}, f32[128,256]{1,0:T(8,128)}, u32[]{:S(2)}) copy-start(f32[128,256]{1,0:T(8,128)} %get-tuple-element.17) | copy-start | bytes 393220

commit v2 on v1

v2 whole, which is shorter than its diff:
```python
import functools

import jax
import jax.numpy as jnp
from jax import lax
from jax.experimental import pallas as pl
from jax.experimental.pallas import tpu as pltpu
from jax.sharding import PartitionSpec as P

MESH = pl.DeviceIdType.MESH
F32 = jnp.float32
BF16 = jnp.bfloat16
ROWS = 128
HALF = 64
SHARE = 16
WIDTH = 256
HEADS = 4
HEAD = 64
NX = 4
PEERS = 16


def dot(a, b):
    return jnp.dot(a, b, preferred_element_type=F32)


def dot_t(a, b):
    return lax.dot_general(a, b, (((1,), (1,)), ((), ())), preferred_element_type=F32)


def kernel(
    nz,
    tans,
    layer_hbm,
    lap_hbm,
    tan_hbm,
    spin_hbm,
    bias_hbm,
    wq_hbm,
    wk_hbm,
    wv_hbm,
    wo_hbm,
    hg_ref,
    sg_ref,
    layer_out,
    tan_out,
    lap_out,
    wq,
    wk,
    wv,
    wo,
    wvt,
    lap_own,
    tan_own,
    g_lb,
    g_t,
    g_s,
    g_x,
    qa,
    ql,
    lhs,
    vt,
    s_bias,
    s_same,
    s_spin,
    top_ref,
    acc,
    sums,
    a_attn,
    a_tan,
    a_term,
    own,
    rs,
    red,
    high,
    ag,
    back_out,
    back_in,
    local_sem,
    d_l_send,
    d_l_recv,
    d_b_send,
    d_b_recv,
    d_s_send,
    d_s_recv,
    y_send,
    y_recv,
    ys_send,
    ys_recv,
    x_send,
    x_recv,
    c_send,
    c_recv,
    t_send,
    t_recv,
    o_send,
    o_recv,
    rs_send,
    rs_recv,
    h_send,
    h_recv,
    ag_send,
    ag_recv,
):
    blk = lax.axis_index("blk")
    tan = lax.axis_index("tan")
    z = blk // 2
    y = blk % 2
    core = tan % 2
    x = (tan // 2) % NX
    high_y = tan // (2 * NX)
    highs = tans // (2 * NX)
    member = core * NX + x
    me = y * (PEERS // 2) + member
    share = pl.ds(pl.multiple_of(member * SHARE, SHARE), SHARE)
    my_half = pl.ds(pl.multiple_of(core * HALF, HALF), HALF)
    own_lanes = pl.ds(pl.multiple_of(y * ROWS, ROWS), ROWS)

    def tan_of(high_at, x_at, core_at):
        return (high_at * NX + x_at) * 2 + core_at

    def group(k):
        at = (me + k) % PEERS
        inner = at % (PEERS // 2)
        return at // (PEERS // 2), inner

    def group_id(k):
        side, inner = group(k)
        return {"blk": z * 2 + side, "tan": tan_of(high_y, inner % NX, inner // NX)}

    def z_id(k):
        return {"blk": ((z + k) % nz) * 2 + y}

    def high_id(k):
        return {"tan": tan_of((high_y + k) % highs, x, core)}

    share_o = tan // 4
    share_y = (tan // 2) % 2
    is_own = tan < 2
    not_own = jnp.logical_not(is_own)
    share_to = ((z + share_o) % nz) * 2 + (y + share_y) % 2
    share_from = ((z + nz - share_o) % nz) * 2 + (y + share_y) % 2

    barrier = pltpu.get_barrier_semaphore()

    def loop(first, last, body):
        def run(k, carry):
            body(k)
            return carry

        lax.fori_loop(first, last, run, 0)

    def greet(device):
        pl.semaphore_signal(barrier, inc=1, device_id=device, device_id_type=MESH)

    loop(1, nz, lambda k: greet(z_id(k)))
    loop(1, PEERS, lambda k: greet(group_id(k)))
    loop(1, highs, lambda k: greet(high_id(k)))

    @pl.when(not_own)
    def _():
        greet({"blk": share_from})

    pair_cols = pl.ds(pl.multiple_of(z * 2 * ROWS, 2 * ROWS), 2 * ROWS)
    local = [
        (tan_hbm.at[y], g_t.at[0, 0]),
        (layer_hbm, g_lb.at[0, 0, 0]),
        (bias_hbm.at[:, pair_cols], g_lb.at[0, 0, 1]),
        (spin_hbm, g_s.at[0, 0]),
        (wq_hbm, wq),
        (wk_hbm, wk),
        (wv_hbm, wv),
        (lap_hbm, lap_own),
        (tan_hbm.at[1 - y], tan_own),
        (wo_hbm, wo),
    ]
    local = [
        pltpu.make_async_copy(src, dst, local_sem.at[n]) for n, (src, dst) in enumerate(local)
    ]
    for copy in local:
        copy.start()

    other_y = {"blk": z * 2 + (1 - y)}
    other_core = {"tan": tan + 1 - 2 * core}
    started = []

    def remote(src, dst, send, recv, device):
        return pltpu.make_async_remote_copy(
            src_ref=src,
            dst_ref=dst,
            send_sem=send,
            recv_sem=recv,
            device_id=device,
            device_id_type=MESH,
        )

    def start(copy):
        copy.start()
        started.append(copy)

    def direct_l(o):
        there = z_id(o)
        return remote(
            layer_hbm.at[share], g_lb.at[o, 0, 0, share], d_l_send.at[o], d_l_recv.at[o], there
        )

    def direct_b(o):
        there = (z + o) % nz
        columns = pl.ds(pl.multiple_of(there * 2 * ROWS, 2 * ROWS), 2 * ROWS)
        return remote(
            bias_hbm.at[share, columns],
            g_lb.at[o, 0, 1, share],
            d_b_send.at[o],
            d_b_recv.at[o],
            z_id(o),
        )

    def direct_s(o):
        return remote(spin_hbm, g_s.at[o, 0], d_s_send.at[o], d_s_recv.at[o], z_id(o))

    def cross(o):
        return remote(
            g_lb.at[o, 0, :, share],
            g_lb.at[o, 1, :, share],
            y_send.at[o],
            y_recv.at[o],
            other_y,
        )

    def cross_s(o):
        return remote(g_s.at[o, 0], g_s.at[o, 1], ys_send.at[o], ys_recv.at[o], other_y)

    def spread(o, k):
        piece = g_lb.at[o, 1, :, share] if o == 0 else g_lb.at[o, :, :, share]
        device = {"tan": tan_of(high_y, (x + k) % NX, core)}
        return remote(piece, piece, x_send.at[o, k], x_recv.at[o, k], device)

    def mate(o):
        piece = g_lb.at[o, 1, :, my_half] if o == 0 else g_lb.at[o, :, :, my_half]
        return remote(piece, piece, c_send.at[o], c_recv.at[o], other_core)

    cross_t = remote(tan_hbm.at[1 - y], g_t.at[0, 1], o_send.at[0], o_recv.at[0], other_y)

    def last_up(side):
        return nz // 2 if side == 0 else nz - 1 - nz // 2

    def flow(o, side):
        if o <= last_up(side):
            src, device = o - 1, z_id(1)
        else:
            src, device = (o + 1) % nz, z_id(nz - 1)
        return remote(
            g_t.at[src, side], g_t.at[o, side], t_send.at[o, side], t_recv.at[o, side], device
        )

    def next_of(o, side):
        last = last_up(side)
        if o == 0:
            return [n for n in sorted({1, nz - 1}) if n <= 1 or n > last]
        if o <= last:
            return [o + 1] if o < last else []
        return [o - 1] if o - 1 > last else []

    def offsets(step):
        return sorted({step, (nz - step) % nz})

    copy_x = remote(lap_hbm.at[my_half], g_x, o_send.at[1], o_recv.at[1], {"blk": share_to})
    copy_x_own = pltpu.make_async_copy(lap_hbm.at[my_half], g_x, local_sem.at[10])

    for copy in local[:4]:
        copy.wait()
    greeted = nz - 1 + PEERS - 1 + highs - 1
    pl.semaphore_wait(barrier, greeted + jnp.where(is_own, 0, 1))

    steps = nz // 2
    start(cross_t)
    start(cross(0))
    start(cross_s(0))
    for step in range(1, steps + 1):
        for o in offsets(step):
            start(direct_l(o))
            start(direct_b(o))
            start(direct_s(o))
        if step == 1:
            for o in next_of(0, 0):
                start(flow(o, 0))

    @pl.when(is_own)
    def _():
        copy_x_own.start()

    @pl.when(not_own)
    def _():
        copy_x.start()

    for copy in local[4:]:
        copy.wait()

    lanes = lax.broadcasted_iota(jnp.int32, (ROWS, ROWS), 1)
    left, right = slice(0, ROWS), slice(ROWS, 2 * ROWS)

    def queries(rows):
        return dot(rows, wq[...]).astype(BF16).astype(F32) * 0.125

    def masked(value, h, scale=1.0):
        pair, e = h // 2, h % 2
        keep = (lanes >= e * HEAD) & (lanes < (e + 1) * HEAD)
        return jnp.where(keep, value[:, pair * ROWS : (pair + 1) * ROWS] * scale, 0.0).astype(BF16)

    zero = jnp.zeros((ROWS, ROWS), BF16)

    def prepare(side):
        at = (y + side) % 2
        q = queries(g_lb[0, side, 0])
        qt = queries(g_t[0, side])

        def rows(n):
            return pl.ds(pl.multiple_of(n * 2 * ROWS + at * ROWS, ROWS), ROWS)

        for h in range(HEADS):
            qh = masked(q, h)
            qa[h, rows(0), left] = qh
            qa[h, rows(0), right] = zero
            qa[h, rows(1), left] = masked(qt, h)
            qa[h, rows(1), right] = qh
            qa[h, rows(2), left] = zero
            qa[h, rows(2), right] = masked(qt, h, 2.0)
        return q

    def prepare_own():
        q = prepare(0)
        qlap = queries(lap_own[...])
        for h in range(HEADS):
            first = slice((h % 2) * ROWS, (h % 2 + 1) * ROWS)
            second = slice((2 + h % 2) * ROWS, (3 + h % 2) * ROWS)
            qh = masked(q, h)
            ql[h // 2, first, left] = qh
            ql[h // 2, first, right] = zero
            ql[h // 2, second, left] = masked(qlap, h)
            ql[h // 2, second, right] = qh
        wvt[...] = jnp.transpose(wv[...].astype(F32)).astype(BF16)
        for h in range(HEADS):
            vt[h, 2 * HEAD :, :] = jnp.ones((16, 2 * ROWS), BF16)
        top_ref[...] = jnp.full(top_ref.shape, -1e30, F32)
        acc[...] = jnp.zeros(acc.shape, F32)
        sums[...] = jnp.zeros(sums.shape, F32)

    def spin_of(o, side):
        return jnp.transpose(jnp.broadcast_to(g_s[o, side].astype(F32), (ROWS, ROWS)))

    def attend(o):
        for n in range(2):
            if n == 0:
                rows = jnp.concatenate([g_lb[o, 0, 0], g_lb[o, 1, 0]], 0)
            else:
                rows = g_t[o].reshape(2 * ROWS, WIDTH)
            keys = dot(rows, wk[...]).astype(BF16)
            for pair in range(2):
                lhs[pair, :, n * ROWS : (n + 1) * ROWS] = keys[:, pair * ROWS : (pair + 1) * ROWS]
            values = dot_t(wvt[...], rows).astype(BF16)
            place = (1 - n) * HEAD
            for h in range(HEADS):
                vt[h, place : place + HEAD, :] = values[h * HEAD : (h + 1) * HEAD]
        for side in range(2):
            rows = slice(side * ROWS, (side + 1) * ROWS)
            s_bias[rows] = g_lb[o, side, 1].astype(F32)
            keys = spin_of(o, side)
            for half in range(2):
                row = g_s[0, (y + half) % 2].astype(F32)
                s_same[rows, half * ROWS : (half + 1) * ROWS] = jnp.where(keys == row, 1.0, 0.0)

        def head_step(h, carry):
            res = dot_t(lhs[h // 2], qa[h])
            wide = 2 * ROWS
            scores = res[:, :wide] + hg_ref[h] * s_bias[...] + sg_ref[h] * s_same[...]
            t, c = res[:, wide : 2 * wide], res[:, 2 * wide :]
            old = top_ref[h]
            top = jnp.maximum(old, jnp.max(scores, axis=0, keepdims=True))
            top_ref[h] = top
            shrink = jnp.exp(old - top)
            expo = jnp.exp(scores - top)
            e1 = expo * t
            e2 = e1 * t + expo * c
            w = expo.astype(BF16)
            w1 = e1.astype(BF16)
            w2 = e2.astype(BF16)
            p = dot(vt[h], jnp.concatenate([w, w1], 1))
            r = dot(vt[h, HEAD:, :], w2)
            a, b = slice(0, 64), slice(64, 128)
            one, two = slice(0, wide), slice(wide, 2 * wide)
            acc[h, 0:64] = acc[h, 0:64] * shrink + p[b, one]
            acc[h, 64:128] = acc[h, 64:128] * shrink + (p[b, two] + p[a, one])
            acc[h, 128:192] = acc[h, 128:192] * shrink + (r[a] + 2.0 * p[a, two])
            sums[h, 0] = sums[h, 0] * shrink + p[128:136, one]
            sums[h, 1] = sums[h, 1] * shrink + p[128:136, two]
            sums[h, 2] = sums[h, 2] * shrink + r[64:72]
            return carry

        lax.fori_loop(0, HEADS, head_step, 0)

    def pass_t(step, side):
        for o in offsets(step):
            if step == 0:
                cross_t.wait_recv()
            else:
                flow(o, side).wait_recv()
            for n in next_of(o, side):
                start(flow(n, side))

    def pass_y(step):
        for o in offsets(step):
            direct_l(o).wait_recv()
            direct_b(o).wait_recv()
            start(cross(o))
            direct_s(o).wait_recv()
            start(cross_s(o))

    def pass_x(step):
        for o in offsets(step):
            cross(o).wait_recv()
            for k in (1, 3, 2):
                start(spread(o, k))

    def pass_core(step):
        for o in offsets(step):
            for k in (1, 3, 2):
                spread(o, k).wait_recv()
            start(mate(o))

    def use(step):
        choices = offsets(step)
        for o in choices:
            cross_s(o).wait_recv()
            mate(o).wait_recv()
        if step == 0:
            prepare(1)
        if len(choices) == 1:
            attend(choices[0])
        else:
            jump = choices[1] - choices[0]

            def one(n, carry):
                attend(choices[0] + n * jump)
                return carry

            lax.fori_loop(0, 2, one, 0)

    pass_t(0, 1)
    prepare_own()
    pass_x(0)
    pass_y(1)
    pass_t(1, 0)
    pass_t(1, 1)
    for step in range(2, steps + 1):
        pass_y(step)
    pass_x(1)
    pass_core(0)
    pass_t(2, 0)
    pass_t(2, 1)
    for step in range(2, steps + 1):
        pass_x(step)
    pass_core(1)
    use(0)
    pass_t(3, 0)
    pass_t(3, 1)
    for step in range(2, steps + 1):
        pass_core(step)
    use(1)
    use(2)
    use(3)
    pass_t(4, 0)
    pass_t(4, 1)
    use(4)

    @pl.when(is_own)
    def _():
        copy_x_own.wait()

    @pl.when(not_own)
    def _():
        copy_x.wait()

    lx = g_lb[share_o, share_y, 0, my_half]
    lk = dot(lx, wk[...]).astype(BF16)
    lv = dot_t(wvt[...], lx).astype(BF16)
    lk2 = dot(g_x[...], wk[...]).astype(BF16)
    lv2 = dot_t(wvt[...], g_x[...]).astype(BF16)
    lbias = g_lb[share_o, share_y, 1, my_half, own_lanes].astype(F32)
    s_spin[...] = jnp.where(spin_of(share_o, share_y) == g_s[0, 0].astype(F32), 1.0, 0.0)
    lsame = s_spin[my_half]
    for h in range(HEADS):
        inv = 1.0 / sums[h, 0, 0:1]
        td = sums[h, 1, 0:1]
        attn = acc[h, 0:64] * inv
        at = (acc[h, 64:128] - attn * td) * inv
        hrows = slice(h * HEAD, (h + 1) * HEAD)
        a_attn[hrows] = attn
        a_tan[hrows] = at
        a_term[hrows] = (acc[h, 128:192] - attn * sums[h, 2, 0:1] - 2.0 * td * at) * inv
    for pair in range(2):
        cols = slice(pair * ROWS, (pair + 1) * ROWS)
        res = dot_t(jnp.concatenate([lk[:, cols], lk2[:, cols]], 1), ql[pair])
        for e in range(2):
            h = pair * 2 + e
            scores = res[:, e * ROWS : (e + 1) * ROWS] + hg_ref[h] * lbias + sg_ref[h] * lsame
            expo = jnp.exp(scores - top_ref[h, :, own_lanes])
            w = expo.astype(BF16)
            wl = (expo * res[:, (2 + e) * ROWS : (3 + e) * ROWS]).astype(BF16)
            hrows = slice(h * HEAD, (h + 1) * HEAD)
            lnum = dot(lv[hrows], wl) + dot(lv2[hrows], w)
            lsum = jnp.sum(wl.astype(F32), axis=0, keepdims=True)
            inv = 1.0 / sums[h, 0, 0:1, own_lanes]
            a_term[hrows, own_lanes] += (lnum - a_attn[hrows, own_lanes] * lsum) * inv

    for side in range(2):
        terms = a_term[:, side * ROWS : (side + 1) * ROWS].astype(BF16)
        own[side] = terms.reshape(PEERS // 2, 2 * SHARE, ROWS)

    def rs_copy(k):
        side, inner = group(k)
        return remote(own.at[side, inner], rs.at[k], rs_send.at[k], rs_recv.at[k], group_id(k))

    def high_copy(k):
        return remote(red, high.at[high_y], h_send.at[k], h_recv.at[k], high_id(k))

    def ag_copy(k):
        inner = (member + k) % (PEERS // 2)
        device = {"tan": tan_of(high_y, inner % NX, inner // NX)}
        return remote(ag.at[member], ag.at[member], ag_send.at[k], ag_recv.at[k], device)

    def project_out(value, rows):
        flat = jnp.transpose(value).astype(BF16)
        return dot(flat, wo[...]) + rows.astype(F32)

    loop(1, PEERS, lambda k: rs_copy(k).start())
    other_lanes = pl.ds(pl.multiple_of((1 - y) * ROWS, ROWS), ROWS)
    back_out[...] = project_out(a_tan[:, other_lanes], g_t[0, 1]).astype(BF16)
    copy_back = remote(back_out, back_in, o_send.at[2], o_recv.at[2], other_y)
    copy_back.start()
    rs[0] = own[y, member]
    loop(1, PEERS, lambda k: rs_copy(k).wait_recv())
    red[...] = jnp.sum(rs[...].astype(F32), axis=0).astype(BF16)
    loop(1, highs, lambda k: high_copy(k).start())
    layer_out[...] = project_out(a_attn[:, own_lanes], g_lb[0, 0, 0]).astype(BF16)
    tan_out[y] = project_out(a_tan[:, own_lanes], g_t[0, 0]).astype(BF16)
    high[high_y] = red[...]
    loop(1, highs, lambda k: high_copy(k).wait_recv())
    ag[member] = jnp.sum(high[...].astype(F32), axis=0).astype(BF16)
    loop(1, PEERS // 2, lambda k: ag_copy(k).start())
    copy_back.wait_recv()
    tan_out[1 - y] = back_in[...]
    for copy in started:
        copy.wait_send()
    copy_back.wait_send()
    loop(1, PEERS, lambda k: rs_copy(k).wait_send())
    loop(1, highs, lambda k: high_copy(k).wait_send())
    loop(1, PEERS // 2, lambda k: ag_copy(k).wait_recv())
    lap_out[...] = project_out(ag[...].reshape(WIDTH, ROWS).astype(F32), lap_own[...])
    loop(1, PEERS // 2, lambda k: ag_copy(k).wait_send())


def solution(mesh):
    blks, tans = mesh.shape["blk"], mesh.shape["tan"]
    nz = blks // 2

    def on_device(layer, lap, tangent, spin, bias, wq, wk, wv, wo, hg, sg):
        tangents = jnp.transpose(tangent, (1, 0, 2))
        spins = spin.reshape(1, ROWS)
        any_spec = pl.BlockSpec(memory_space=pl.ANY)
        smem = pl.BlockSpec(memory_space=pltpu.SMEM)
        vmem = pl.BlockSpec(memory_space=pltpu.VMEM)
        sq = (WIDTH, WIDTH)
        scratch = [
            pltpu.VMEM(sq, BF16),
            pltpu.VMEM(sq, BF16),
            pltpu.VMEM(sq, BF16),
            pltpu.VMEM(sq, BF16),
            pltpu.VMEM(sq, BF16),
            pltpu.VMEM((ROWS, WIDTH), BF16),
            pltpu.VMEM((ROWS, WIDTH), BF16),
            pltpu.VMEM((nz, 2, 2, ROWS, WIDTH), BF16),
            pltpu.VMEM((nz, 2, ROWS, WIDTH), BF16),
            pltpu.VMEM((nz, 2, 1, ROWS), jnp.int32),
            pltpu.VMEM((HALF, WIDTH), BF16),
            pltpu.VMEM((HEADS, 6 * ROWS, WIDTH), BF16),
            pltpu.VMEM((2, 4 * ROWS, WIDTH), BF16),
            pltpu.VMEM((2, 2 * ROWS, WIDTH), BF16),
            pltpu.VMEM((HEADS, 2 * HEAD + 16, 2 * ROWS), BF16),
            pltpu.VMEM((2 * ROWS, 2 * ROWS), F32),
            pltpu.VMEM((2 * ROWS, 2 * ROWS), F32),
            pltpu.VMEM((ROWS, ROWS), F32),
            pltpu.VMEM((HEADS, 1, 2 * ROWS), F32),
            pltpu.VMEM((HEADS, 3 * HEAD, 2 * ROWS), F32),
            pltpu.VMEM((HEADS, 3, 8, 2 * ROWS), F32),
            pltpu.VMEM((WIDTH, 2 * ROWS), F32),
            pltpu.VMEM((WIDTH, 2 * ROWS), F32),
            pltpu.VMEM((WIDTH, 2 * ROWS), F32),
            pltpu.VMEM((2, PEERS // 2, 2 * SHARE, ROWS), BF16),
            pltpu.VMEM((PEERS, 2 * SHARE, ROWS), BF16),
            pltpu.VMEM((2 * SHARE, ROWS), BF16),
            pltpu.VMEM((tans // (2 * NX), 2 * SHARE, ROWS), BF16),
            pltpu.VMEM((PEERS // 2, 2 * SHARE, ROWS), BF16),
            pltpu.VMEM((ROWS, WIDTH), BF16),
            pltpu.VMEM((ROWS, WIDTH), BF16),
            pltpu.SemaphoreType.DMA((11,)),
        ]
        one, two = (nz,), (nz, 2)
        shapes = (one, one, one, one, one, (nz, NX), one, two, (3,))
        for shape in shapes + ((PEERS,), (tans // (2 * NX),), (PEERS // 2,)):
            scratch += [pltpu.SemaphoreType.DMA(shape)] * 2
        layer_out, tan_out, lap_out = pl.pallas_call(
            functools.partial(kernel, nz, tans),
            out_shape=(
                jax.ShapeDtypeStruct((ROWS, WIDTH), BF16),
                jax.ShapeDtypeStruct((2, ROWS, WIDTH), BF16),
                jax.ShapeDtypeStruct((ROWS, WIDTH), F32),
            ),
            in_specs=[any_spec] * 9 + [smem, smem],
            out_specs=(vmem, vmem, vmem),
            scratch_shapes=scratch,
            compiler_params=pltpu.CompilerParams(collective_id=0, has_side_effects=True),
            name="laplacian_attention",
        )(layer, lap, tangents, spins, bias, wq, wk, wv, wo, hg, sg)
        return layer_out, jnp.transpose(tan_out, (1, 0, 2)), lap_out

    in_specs = (
        P("blk", None),
        P("blk", None),
        P("blk", "tan", None),
        P("blk"),
        P("blk", None),
        P(),
        P(),
        P(),
        P(),
        P(),
        P(),
    )
    out_specs = (P("blk", None), P("blk", "tan", None), P("blk", None))
    return jax.shard_map(
        on_device, mesh=mesh, in_specs=in_specs, out_specs=out_specs, check_vma=False
    )
```

time: 80.8 us -> 80 us (0.990)
  other arithmetic: 1.17 us -> 0 us
    reshape x1 -> x0, other arithmetic: 1.17 us -> none  [on_device(): spins = spin.astype(F32).reshape(1, ROWS)]
where the time goes in v2:
time: 80 us; the launch traced here: 79.8 us
  Pallas kernels  74.2 us (93%)
  local copies, waits for them, and re-layouts  4.89 us (6%)
    pallas_call x1, Pallas kernels, on_device(): pl.pallas_call(functools.partial(kernel, nz, tans), out_shape=(jax.ShapeD...  74.2 us
    unnamed x8, local copies, waits for them, and re-layouts  4.89 us

profile of v2, /device:TPU:1, one launch (start us, length us, event | category | flops | bytes accessed | tf_op | source)
XLA Modules:
  0.0 79.8 jit_solution(6773153365891574223)
XLA Ops:
  0.6 1.6 %copy.17 = bf16[128,2,256]{2,0,1:T(8,128)(2,1)} copy(bf16[128,2,256]{2,1,0:T(2,128)(2,1)} %param.13) | data formatting | bytes 262144 | tf_op args[2]
  2.2 74.2 %laplacian_attention.1 = (bf16[128,256]{1,0:T(8,128)(2,1)}, bf16[2,128,256]{2,1,0:T(8,128)(2,1)}, f32[128,256]{1,0:T(8,128)}) custom-call(bf16[128,256]{1,0:T(8,128)(2,1)} %layer_hbm.1, bf16[128,256]{1,0:T(8,128)(2,1)} %lap_hbm.1, bf16[2,128,256]{2,1,0:T(8,128)(2,1)} %bitcast.5, s32[1,128]{1,0:T(1,128)} %bitcast.7, bf16[128,2048]{1,0:T(8,128)(2,1)} %bias_hbm.1, ...), custom_call_target="tpu_custom_call" | custom-call | tf_op jit(solution)/shard_map/laplacian_attention/pallas_call | solution.py:611
  76.4 0.0 copy-start.1
  76.5 1.7 %copy.15 = bf16[128,2,256]{2,1,0:T(2,128)(2,1)} copy(bf16[128,2,256]{2,0,1:T(8,128)(2,1)} %bitcast.6) | data formatting | bytes 262144
  78.2 0.0 copy-done.1
  78.2 0.0 copy-start
  78.2 0.6 copy.20
  78.8 0.3 copy-done
  79.1 0.7 copy.21
Async XLA Ops:
  76.4 1.7 %copy-start.1 = (bf16[128,256]{1,0:T(8,128)(2,1)S(1)}, bf16[128,256]{1,0:T(8,128)(2,1)}, u32[]{:S(2)}) copy-start(bf16[128,256]{1,0:T(8,128)(2,1)} %get-tuple-element.15) | copy-start | bytes 196612
  78.2 0.9 %copy-start = (f32[128,256]{1,0:T(8,128)S(1)}, f32[128,256]{1,0:T(8,128)}, u32[]{:S(2)}) copy-start(f32[128,256]{1,0:T(8,128)} %get-tuple-element.17) | copy-start | bytes 393220

commit v3 on v2

--- a/solution.py
+++ b/solution.py
@@ -52,6 +52,7 @@
     wvt,
     lap_own,
     tan_own,
+    tan_raw,
     g_lb,
     g_t,
     g_s,
@@ -61,6 +62,8 @@
     lhs,
     vt,
     s_bias,
+    s_score,
+    s_w,
     s_same,
     s_spin,
     top_ref,
@@ -163,7 +166,7 @@
 
     pair_cols = pl.ds(pl.multiple_of(z * 2 * ROWS, 2 * ROWS), 2 * ROWS)
     local = [
-        (tan_hbm.at[y], g_t.at[0, 0]),
+        (tan_hbm, tan_raw),
         (layer_hbm, g_lb.at[0, 0, 0]),
         (bias_hbm.at[:, pair_cols], g_lb.at[0, 0, 1]),
         (spin_hbm, g_s.at[0, 0]),
@@ -171,7 +174,6 @@
         (wk_hbm, wk),
         (wv_hbm, wv),
         (lap_hbm, lap_own),
-        (tan_hbm.at[1 - y], tan_own),
         (wo_hbm, wo),
     ]
     local = [
@@ -219,6 +221,8 @@
         return remote(spin_hbm, g_s.at[o, 0], d_s_send.at[o], d_s_recv.at[o], z_id(o))
 
     def cross(o):
+        if o == 0:
+            return remote(g_lb.at[0, 0], g_lb.at[0, 1], y_send.at[0], y_recv.at[0], other_y)
         return remote(
             g_lb.at[o, 0, :, share],
             g_lb.at[o, 1, :, share],
@@ -231,15 +235,15 @@
         return remote(g_s.at[o, 0], g_s.at[o, 1], ys_send.at[o], ys_recv.at[o], other_y)
 
     def spread(o, k):
-        piece = g_lb.at[o, 1, :, share] if o == 0 else g_lb.at[o, :, :, share]
+        piece = g_lb.at[o, :, :, share]
         device = {"tan": tan_of(high_y, (x + k) % NX, core)}
         return remote(piece, piece, x_send.at[o, k], x_recv.at[o, k], device)
 
     def mate(o):
-        piece = g_lb.at[o, 1, :, my_half] if o == 0 else g_lb.at[o, :, :, my_half]
+        piece = g_lb.at[o, :, :, my_half]
         return remote(piece, piece, c_send.at[o], c_recv.at[o], other_core)
 
-    cross_t = remote(tan_hbm.at[1 - y], g_t.at[0, 1], o_send.at[0], o_recv.at[0], other_y)
+    cross_t = remote(tan_own, g_t.at[0, 1], o_send.at[0], o_recv.at[0], other_y)
 
     def last_up(side):
         return nz // 2 if side == 0 else nz - 1 - nz // 2
@@ -265,10 +269,14 @@
         return sorted({step, (nz - step) % nz})
 
     copy_x = remote(lap_hbm.at[my_half], g_x, o_send.at[1], o_recv.at[1], {"blk": share_to})
-    copy_x_own = pltpu.make_async_copy(lap_hbm.at[my_half], g_x, local_sem.at[10])
+    copy_x_own = pltpu.make_async_copy(lap_hbm.at[my_half], g_x, local_sem.at[9])
 
     for copy in local[:4]:
         copy.wait()
+    raw = tan_raw[...].astype(F32)
+    first, second = raw[:, 0].astype(BF16), raw[:, 1].astype(BF16)
+    g_t[0, 0] = jnp.where(y == 0, first, second)
+    tan_own[...] = jnp.where(y == 0, second, first)
     greeted = nz - 1 + PEERS - 1 + highs - 1
     pl.semaphore_wait(barrier, greeted + jnp.where(is_own, 0, 1))
 
@@ -348,7 +356,7 @@
     def spin_of(o, side):
         return jnp.transpose(jnp.broadcast_to(g_s[o, side].astype(F32), (ROWS, ROWS)))
 
-    def attend(o):
+    def attend_front(o):
         for n in range(2):
             if n == 0:
                 rows = jnp.concatenate([g_lb[o, 0, 0], g_lb[o, 1, 0]], 0)
@@ -369,23 +377,27 @@
                 row = g_s[0, (y + half) % 2].astype(F32)
                 s_same[rows, half * ROWS : (half + 1) * ROWS] = jnp.where(keys == row, 1.0, 0.0)
 
+    def attend_heads(heads):
         def head_step(h, carry):
-            res = dot_t(lhs[h // 2], qa[h])
             wide = 2 * ROWS
-            scores = res[:, :wide] + hg_ref[h] * s_bias[...] + sg_ref[h] * s_same[...]
-            t, c = res[:, wide : 2 * wide], res[:, 2 * wide :]
+            keys = lhs[h // 2]
+            first = dot_t(keys, qa[h, :wide])
+            s_score[h % 2] = first + (hg_ref[h] * s_bias[...] + sg_ref[h] * s_same[...])
             old = top_ref[h]
-            top = jnp.maximum(old, jnp.max(scores, axis=0, keepdims=True))
+            top = jnp.maximum(old, jnp.max(s_score[h % 2], axis=0, keepdims=True))
             top_ref[h] = top
             shrink = jnp.exp(old - top)
-            expo = jnp.exp(scores - top)
-            e1 = expo * t
-            e2 = e1 * t + expo * c
-            w = expo.astype(BF16)
-            w1 = e1.astype(BF16)
-            w2 = e2.astype(BF16)
-            p = dot(vt[h], jnp.concatenate([w, w1], 1))
-            r = dot(vt[h, HEAD:, :], w2)
+            for n in range(wide // 256):
+                part = slice(n * 256, (n + 1) * 256)
+                expo = jnp.exp(s_score[h % 2, part] - top)
+                s_w[h % 2, part, :wide] = expo.astype(BF16)
+                tc = dot_t(lhs[h // 2, part], qa[h, wide:])
+                t, c = tc[:, :wide], tc[:, wide:]
+                e1 = expo * t
+                s_w[h % 2, part, wide : 2 * wide] = e1.astype(BF16)
+                s_w[h % 2, part, 2 * wide :] = (e1 * t + expo * c).astype(BF16)
+            p = dot(vt[h], s_w[h % 2, :, : 2 * wide])
+            r = dot(vt[h, HEAD:, :], s_w[h % 2, :, 2 * wide :])
             a, b = slice(0, 64), slice(64, 128)
             one, two = slice(0, wide), slice(wide, 2 * wide)
             acc[h, 0:64] = acc[h, 0:64] * shrink + p[b, one]
@@ -396,7 +408,8 @@
             sums[h, 2] = sums[h, 2] * shrink + r[64:72]
             return carry
 
-        lax.fori_loop(0, HEADS, head_step, 0)
+        for h in heads:
+            head_step(h, 0)
 
     def pass_t(step, side):
         for o in offsets(step):
@@ -427,50 +440,45 @@
                 spread(o, k).wait_recv()
             start(mate(o))
 
-    def use(step):
-        choices = offsets(step)
-        for o in choices:
-            cross_s(o).wait_recv()
-            mate(o).wait_recv()
-        if step == 0:
+    def landed(o):
+        cross_s(o).wait_recv()
+        mate(o).wait_recv()
+
+    def attend(o, between=()):
+        if o == 0:
+            cross(0).wait_recv()
+            cross_s(0).wait_recv()
             prepare(1)
-        if len(choices) == 1:
-            attend(choices[0])
-        else:
-            jump = choices[1] - choices[0]
-
-            def one(n, carry):
-                attend(choices[0] + n * jump)
-                return carry
-
-            lax.fori_loop(0, 2, one, 0)
-
+        elif o != nz // 2:
+            landed(o)
+        attend_front(o)
+        attend_heads((0, 1))
+        for call, *args in between:
+            call(*args)
+        attend_heads((2, 3))
+
+    prepare_own()
     pass_t(0, 1)
-    prepare_own()
-    pass_x(0)
     pass_y(1)
     pass_t(1, 0)
+    pass_y(2)
+    pass_x(1)
     pass_t(1, 1)
-    for step in range(2, steps + 1):
-        pass_y(step)
-    pass_x(1)
-    pass_core(0)
-    pass_t(2, 0)
+    pass_y(3)
+    attend(0, ((pass_x, 2), (pass_y, 4), (pass_t, 2, 0)))
+    pass_core(1)
+    pass_x(3)
     pass_t(2, 1)
-    for step in range(2, steps + 1):
-        pass_x(step)
-    pass_core(1)
-    use(0)
-    pass_t(3, 0)
+    pass_x(4)
+    attend(1, ((pass_core, 2), (pass_t, 3, 0)))
     pass_t(3, 1)
-    for step in range(2, steps + 1):
-        pass_core(step)
-    use(1)
-    use(2)
-    use(3)
-    pass_t(4, 0)
-    pass_t(4, 1)
-    use(4)
+    attend(7, ((pass_core, 3),))
+    pass_core(4)
+    attend(2)
+    attend(6)
+    attend(3)
+    attend(5)
+    landed(nz // 2)
 
     @pl.when(is_own)
     def _():
@@ -488,6 +496,19 @@
     lbias = g_lb[share_o, share_y, 1, my_half, own_lanes].astype(F32)
     s_spin[...] = jnp.where(spin_of(share_o, share_y) == g_s[0, 0].astype(F32), 1.0, 0.0)
     lsame = s_spin[my_half]
+    lap_scores = []
+    for pair in range(2):
+        cols = slice(pair * ROWS, (pair + 1) * ROWS)
+        res = dot_t(jnp.concatenate([lk[:, cols], lk2[:, cols]], 1), ql[pair])
+        for e in range(2):
+            h = pair * 2 + e
+            scores = res[:, e * ROWS : (e + 1) * ROWS] + hg_ref[h] * lbias + sg_ref[h] * lsame
+            lap_scores.append((scores, res[:, (2 + e) * ROWS : (3 + e) * ROWS]))
+    pass_t(4, 0)
+    pass_t(4, 1)
+    attend(4)
+
+
     for h in range(HEADS):
         inv = 1.0 / sums[h, 0, 0:1]
         td = sums[h, 1, 0:1]
@@ -497,20 +518,16 @@
         a_attn[hrows] = attn
         a_tan[hrows] = at
         a_term[hrows] = (acc[h, 128:192] - attn * sums[h, 2, 0:1] - 2.0 * td * at) * inv
-    for pair in range(2):
-        cols = slice(pair * ROWS, (pair + 1) * ROWS)
-        res = dot_t(jnp.concatenate([lk[:, cols], lk2[:, cols]], 1), ql[pair])
-        for e in range(2):
-            h = pair * 2 + e
-            scores = res[:, e * ROWS : (e + 1) * ROWS] + hg_ref[h] * lbias + sg_ref[h] * lsame
-            expo = jnp.exp(scores - top_ref[h, :, own_lanes])
-            w = expo.astype(BF16)
-            wl = (expo * res[:, (2 + e) * ROWS : (3 + e) * ROWS]).astype(BF16)
-            hrows = slice(h * HEAD, (h + 1) * HEAD)
-            lnum = dot(lv[hrows], wl) + dot(lv2[hrows], w)
-            lsum = jnp.sum(wl.astype(F32), axis=0, keepdims=True)
-            inv = 1.0 / sums[h, 0, 0:1, own_lanes]
-            a_term[hrows, own_lanes] += (lnum - a_attn[hrows, own_lanes] * lsum) * inv
+    for h in range(HEADS):
+        scores, changes = lap_scores[h]
+        expo = jnp.exp(scores - top_ref[h, :, own_lanes])
+        w = expo.astype(BF16)
+        wl = (expo * changes).astype(BF16)
+        hrows = slice(h * HEAD, (h + 1) * HEAD)
+        lnum = dot(lv[hrows], wl) + dot(lv2[hrows], w)
+        lsum = jnp.sum(wl.astype(F32), axis=0, keepdims=True)
+        inv = 1.0 / sums[h, 0, 0:1, own_lanes]
+        a_term[hrows, own_lanes] += (lnum - a_attn[hrows, own_lanes] * lsum) * inv
 
     for side in range(2):
         terms = a_term[:, side * ROWS : (side + 1) * ROWS].astype(BF16)
@@ -542,13 +559,15 @@
     red[...] = jnp.sum(rs[...].astype(F32), axis=0).astype(BF16)
     loop(1, highs, lambda k: high_copy(k).start())
     layer_out[...] = project_out(a_attn[:, own_lanes], g_lb[0, 0, 0]).astype(BF16)
-    tan_out[y] = project_out(a_tan[:, own_lanes], g_t[0, 0]).astype(BF16)
+    mine = project_out(a_tan[:, own_lanes], g_t[0, 0])
     high[high_y] = red[...]
     loop(1, highs, lambda k: high_copy(k).wait_recv())
     ag[member] = jnp.sum(high[...].astype(F32), axis=0).astype(BF16)
     loop(1, PEERS // 2, lambda k: ag_copy(k).start())
     copy_back.wait_recv()
-    tan_out[1 - y] = back_in[...]
+    theirs = back_in[...].astype(F32)
+    tan_out[:, 0] = jnp.where(y == 0, mine, theirs).astype(BF16)
+    tan_out[:, 1] = jnp.where(y == 0, theirs, mine).astype(BF16)
     for copy in started:
         copy.wait_send()
     copy_back.wait_send()
@@ -564,7 +583,6 @@
     nz = blks // 2
 
     def on_device(layer, lap, tangent, spin, bias, wq, wk, wv, wo, hg, sg):
-        tangents = jnp.transpose(tangent, (1, 0, 2))
         spins = spin.reshape(1, ROWS)
         any_spec = pl.BlockSpec(memory_space=pl.ANY)
         smem = pl.BlockSpec(memory_space=pltpu.SMEM)
@@ -578,6 +596,7 @@
             pltpu.VMEM(sq, BF16),
             pltpu.VMEM((ROWS, WIDTH), BF16),
             pltpu.VMEM((ROWS, WIDTH), BF16),
+            pltpu.VMEM((ROWS, 2, WIDTH), BF16),
             pltpu.VMEM((nz, 2, 2, ROWS, WIDTH), BF16),
             pltpu.VMEM((nz, 2, ROWS, WIDTH), BF16),
             pltpu.VMEM((nz, 2, 1, ROWS), jnp.int32),
@@ -587,6 +606,8 @@
             pltpu.VMEM((2, 2 * ROWS, WIDTH), BF16),
             pltpu.VMEM((HEADS, 2 * HEAD + 16, 2 * ROWS), BF16),
             pltpu.VMEM((2 * ROWS, 2 * ROWS), F32),
+            pltpu.VMEM((2, 2 * ROWS, 2 * ROWS), F32),
+            pltpu.VMEM((2, 2 * ROWS, 6 * ROWS), BF16),
             pltpu.VMEM((2 * ROWS, 2 * ROWS), F32),
             pltpu.VMEM((ROWS, ROWS), F32),
             pltpu.VMEM((HEADS, 1, 2 * ROWS), F32),
@@ -612,7 +633,7 @@
             functools.partial(kernel, nz, tans),
             out_shape=(
                 jax.ShapeDtypeStruct((ROWS, WIDTH), BF16),
-                jax.ShapeDtypeStruct((2, ROWS, WIDTH), BF16),
+                jax.ShapeDtypeStruct((ROWS, 2, WIDTH), BF16),
                 jax.ShapeDtypeStruct((ROWS, WIDTH), F32),
             ),
             in_specs=[any_spec] * 9 + [smem, smem],
@@ -620,8 +641,8 @@
             scratch_shapes=scratch,
             compiler_params=pltpu.CompilerParams(collective_id=0, has_side_effects=True),
             name="laplacian_attention",
-        )(layer, lap, tangents, spins, bias, wq, wk, wv, wo, hg, sg)
-        return layer_out, jnp.transpose(tan_out, (1, 0, 2)), lap_out
+        )(layer, lap, tangent, spins, bias, wq, wk, wv, wo, hg, sg)
+        return layer_out, tan_out, lap_out
 
     in_specs = (
         P("blk", None),

time: 80 us -> 67.6 us (0.84)
  Pallas kernels: 74.2 us -> 63.7 us
  local copies, waits for them, and re-layouts: 4.89 us -> 3.12 us
    pallas_call x1, Pallas kernels: 74.2 us -> 63.7 us  [on_device(): pl.pallas_call(functools.partial(kernel, nz, tans), out_shape=(jax.ShapeD...]
    unnamed x8 -> x7, local copies, waits for them, and re-layouts: 4.89 us -> 3.12 us
where the time goes in v3:
time: 67.6 us; the launch traced here: 67.4 us
  Pallas kernels  63.7 us (94%)
  local copies, waits for them, and re-layouts  3.12 us (5%)
    pallas_call x1, Pallas kernels, on_device(): pl.pallas_call(functools.partial(kernel, nz, tans), out_shape=(jax.ShapeD...  63.7 us
    unnamed x7, local copies, waits for them, and re-layouts  3.12 us

profile of v3, /device:TPU:1, one launch (start us, length us, event | category | flops | bytes accessed | tf_op | source)
XLA Modules:
  0.0 67.4 jit_solution(18219210555386462947)
XLA Ops:
  0.6 63.7 %laplacian_attention.1 = (bf16[128,256]{1,0:T(8,128)(2,1)}, bf16[128,2,256]{2,1,0:T(2,128)(2,1)}, f32[128,256]{1,0:T(8,128)}) custom-call(bf16[128,256]{1,0:T(8,128)(2,1)} %layer_hbm.1, bf16[128,256]{1,0:T(8,128)(2,1)} %lap_hbm.1, bf16[128,2,256]{2,1,0:T(2,128)(2,1)} %tan_hbm.1, s32[1,128]{1,0:T(1,128)} %bitcast.1, bf16[128,2048]{1,0:T(8,128)(2,1)} %bias_hbm.1, ...), custom_call_target="tpu_custom_call" | custom-call | tf_op jit(solution)/shard_map/laplacian_attention/pallas_call | solution.py:632
  64.3 0.0 copy-start.1
  64.3 1.5 %copy.17 = bf16[128,256]{1,0:T(8,128)(2,1)} copy(bf16[128,256]{1,0:T(8,128)(2,1)} %get-tuple-element.6) | data formatting | bytes 131072
  65.8 0.0 copy-done.1
  65.8 0.0 copy-start
  65.8 0.7 copy.18
  66.5 0.3 copy-done
  66.8 0.7 copy.19
Async XLA Ops:
  64.3 1.5 %copy-start.1 = (bf16[128,2,256]{2,1,0:T(2,128)(2,1)S(1)}, bf16[128,2,256]{2,1,0:T(2,128)(2,1)}, u32[]{:S(2)}) copy-start(bf16[128,2,256]{2,1,0:T(2,128)(2,1)} %get-tuple-element.7) | copy-start | bytes 393220
  65.8 1.0 %copy-start = (f32[128,256]{1,0:T(8,128)S(1)}, f32[128,256]{1,0:T(8,128)}, u32[]{:S(2)}) copy-start(f32[128,256]{1,0:T(8,128)} %get-tuple-element.8) | copy-start | bytes 393220

commit v4 on v3

--- a/solution.py
+++ b/solution.py
@@ -234,10 +234,10 @@
     def cross_s(o):
         return remote(g_s.at[o, 0], g_s.at[o, 1], ys_send.at[o], ys_recv.at[o], other_y)
 
-    def spread(o, k):
-        piece = g_lb.at[o, :, :, share]
+    def spread(o, side, k):
+        piece = g_lb.at[o, side, :, share]
         device = {"tan": tan_of(high_y, (x + k) % NX, core)}
-        return remote(piece, piece, x_send.at[o, k], x_recv.at[o, k], device)
+        return remote(piece, piece, x_send.at[o, side, k], x_recv.at[o, side, k], device)
 
     def mate(o):
         piece = g_lb.at[o, :, :, my_half]
@@ -425,6 +425,8 @@
             direct_l(o).wait_recv()
             direct_b(o).wait_recv()
             start(cross(o))
+            for k in (1, 3, 2):
+                start(spread(o, 0, k))
             direct_s(o).wait_recv()
             start(cross_s(o))
 
@@ -432,12 +434,13 @@
         for o in offsets(step):
             cross(o).wait_recv()
             for k in (1, 3, 2):
-                start(spread(o, k))
+                start(spread(o, 1, k))
 
     def pass_core(step):
         for o in offsets(step):
-            for k in (1, 3, 2):
-                spread(o, k).wait_recv()
+            for side in range(2):
+                for k in (1, 3, 2):
+                    spread(o, side, k).wait_recv()
             start(mate(o))
 
     def landed(o):
@@ -470,12 +473,10 @@
     pass_x(3)
     pass_t(2, 1)
     pass_x(4)
-    attend(1, ((pass_core, 2), (pass_t, 3, 0)))
-    pass_t(3, 1)
+    attend(1, ((pass_core, 2),))
     attend(7, ((pass_core, 3),))
-    pass_core(4)
-    attend(2)
-    attend(6)
+    attend(2, ((pass_t, 3, 0),))
+    attend(6, ((pass_t, 3, 1), (pass_core, 4)))
     attend(3)
     attend(5)
     landed(nz // 2)
@@ -626,7 +627,7 @@
             pltpu.SemaphoreType.DMA((11,)),
         ]
         one, two = (nz,), (nz, 2)
-        shapes = (one, one, one, one, one, (nz, NX), one, two, (3,))
+        shapes = (one, one, one, one, one, (nz, 2, NX), one, two, (3,))
         for shape in shapes + ((PEERS,), (tans // (2 * NX),), (PEERS // 2,)):
             scratch += [pltpu.SemaphoreType.DMA(shape)] * 2
         layer_out, tan_out, lap_out = pl.pallas_call(

time: 67.6 us -> 67.5 us (level)
  no operation moved by 1% of the time
where the time goes in v4:
time: 67.5 us; the launch traced here: 67.3 us
  Pallas kernels  63.5 us (94%)
  local copies, waits for them, and re-layouts  3.12 us (5%)
    pallas_call x1, Pallas kernels, on_device(): pl.pallas_call(functools.partial(kernel, nz, tans), out_shape=(jax.ShapeD...  63.5 us
    unnamed x7, local copies, waits for them, and re-layouts  3.12 us

profile of v4, /device:TPU:1, one launch (start us, length us, event | category | flops | bytes accessed | tf_op | source)
XLA Modules:
  0.0 67.3 jit_solution(9153305014668020169)
XLA Ops:
  0.6 63.5 %laplacian_attention.1 = (bf16[128,256]{1,0:T(8,128)(2,1)}, bf16[128,2,256]{2,1,0:T(2,128)(2,1)}, f32[128,256]{1,0:T(8,128)}) custom-call(bf16[128,256]{1,0:T(8,128)(2,1)} %layer_hbm.1, bf16[128,256]{1,0:T(8,128)(2,1)} %lap_hbm.1, bf16[128,2,256]{2,1,0:T(2,128)(2,1)} %tan_hbm.1, s32[1,128]{1,0:T(1,128)} %bitcast.1, bf16[128,2048]{1,0:T(8,128)(2,1)} %bias_hbm.1, ...), custom_call_target="tpu_custom_call" | custom-call | tf_op jit(solution)/shard_map/laplacian_attention/pallas_call | solution.py:633
  64.2 0.0 copy-start.1
  64.2 1.5 %copy.17 = bf16[128,256]{1,0:T(8,128)(2,1)} copy(bf16[128,256]{1,0:T(8,128)(2,1)} %get-tuple-element.6) | data formatting | bytes 131072
  65.7 0.0 copy-done.1
  65.7 0.0 copy-start
  65.7 0.7 copy.18
  66.4 0.3 copy-done
  66.7 0.7 copy.19
Async XLA Ops:
  64.2 1.5 %copy-start.1 = (bf16[128,2,256]{2,1,0:T(2,128)(2,1)S(1)}, bf16[128,2,256]{2,1,0:T(2,128)(2,1)}, u32[]{:S(2)}) copy-start(bf16[128,2,256]{2,1,0:T(2,128)(2,1)} %get-tuple-element.7) | copy-start | bytes 393220
  65.7 1.0 %copy-start = (f32[128,256]{1,0:T(8,128)S(1)}, f32[128,256]{1,0:T(8,128)}, u32[]{:S(2)}) copy-start(f32[128,256]{1,0:T(8,128)} %get-tuple-element.8) | copy-start | bytes 393220
